TPU v7x, 256 devices: a whole 4x4x8 slice. The times are simulated.
256 devices in a mesh: dp: 8 (over z_hi, core), seq: 32 (over x, z_lo, y).
Axes of the slice: x: 4, y: 4, z: 8 (z_hi: 4, z_lo: 2; z = z_hi * 2 + z_lo), core: 2. Of those that a mesh axis runs over, the one named last changes fastest.
Arguments:
- saved_mixed: bfloat16 [8, 65536, 512], P('dp', 'seq'), may hold values from -6 to 6
- out_grad: bfloat16 [8, 65536, 512], P('dp', 'seq'), may hold values from -6 to 6
- weight_in: bfloat16 [2048, 128], P('dp'), may hold values from -0.5 to 0.5
- weight_out: bfloat16 [2048, 128], P('dp'), may hold values from -0.25 to 0.25
- outer_factor: bfloat16 [256, 256], P('dp'), may hold values from -0.375 to 0.375
- inner_factor: bfloat16 [256, 256], P('dp'), may hold values from -0.375 to 0.375
- twiddle: float32 [256, 256], P(None, 'seq'), may hold values from 0.5 to 2
Outputs:
- input_grad: bfloat16 [8, 65536, 512], P('dp', 'seq')
- weight_in_grad: float32 [2048, 128], P('dp')
- weight_out_grad: float32 [2048, 128], P('dp')
All inputs are finite; a program needn't handle non-finite values.
Results may differ from a plain program's by a relative error of at most 0.0062.
Values may be sent and summed in bfloat16 or wider, within the bound.
No kernel may reach another device: no remote copies, remote signals or barrier semaphores. Data moves between devices by JAX's collectives and lax.ppermute only.
A program may use at most 128 MiB of HBM per device.

v0:
```python
import math

import jax
import jax.numpy as jnp
from jax import lax
from jax.sharding import PartitionSpec as P

NB = 4


def gelu_parts(pre_act):
    coeff = math.sqrt(2.0 / math.pi)
    squared = pre_act * pre_act
    tangent = jnp.tanh(coeff * (pre_act + 0.044715 * squared * pre_act))
    activated = 0.5 * pre_act * (1.0 + tangent)
    slope = 0.5 * (1.0 + tangent) + 0.5 * pre_act * (1.0 - tangent * tangent) * coeff * (
        1.0 + 3.0 * 0.044715 * squared
    )
    return (activated, slope)


def token_product(left_rows, right_rows):
    return lax.dot_general(
        left_rows, right_rows, (((0,), (0,)), ((), ())), preferred_element_type=jnp.float32
    )


def width_product(left_rows, right_rows):
    return lax.dot_general(
        left_rows, right_rows, (((1,), (1,)), ((), ())), preferred_element_type=jnp.float32
    )


def shards(saved_mixed, out_grad, weight_in, weight_out, outer_factor, inner_factor, twiddle):
    data_devices = lax.axis_size("dp")
    seq_devices = lax.axis_size("seq")
    weight_in, weight_out, outer_factor, inner_factor = (
        lax.all_gather(weight_in, "dp", axis=0, tiled=True),
        lax.all_gather(weight_out, "dp", axis=0, tiled=True),
        lax.all_gather(outer_factor, "dp", axis=0, tiled=True),
        lax.all_gather(inner_factor, "dp", axis=0, tiled=True),
    )
    seq_count, row_count, features = saved_mixed.shape
    sub_width = features // NB
    hidden_block = weight_in.shape[0] // NB
    inner_size = inner_factor.shape[0]
    local_outer = row_count // inner_size
    scale_factor = 1.0 / math.sqrt(seq_count * data_devices * row_count * seq_devices)
    saved_tokens = saved_mixed.reshape(seq_count * row_count, features)
    upstream = out_grad.reshape(seq_count * row_count, features)
    input_parts = []
    output_parts = []
    delta_parts = []
    for block_id in range(NB):
        saved_block = saved_tokens[:, block_id * sub_width : (block_id + 1) * sub_width]
        upstream_block = upstream[:, block_id * sub_width : (block_id + 1) * sub_width]
        w_in_block = weight_in[block_id * hidden_block : (block_id + 1) * hidden_block]
        w_out_block = weight_out[block_id * hidden_block : (block_id + 1) * hidden_block]
        pre_act = width_product(saved_block, w_in_block)
        activated, gelu_slope = gelu_parts(pre_act)
        activated = activated.astype(jnp.bfloat16)
        act_grad = width_product(upstream_block, w_out_block)
        pre_grad = (act_grad * gelu_slope).astype(jnp.bfloat16)
        output_parts.append(token_product(activated, upstream_block))
        input_parts.append(token_product(pre_grad, saved_block))
        projected = jnp.dot(pre_grad, w_in_block, preferred_element_type=jnp.float32)
        delta_parts.append((upstream_block.astype(jnp.float32) + projected).astype(jnp.bfloat16))
    grad_in_local = jnp.concatenate(input_parts, axis=0) * scale_factor
    grad_out_local = jnp.concatenate(output_parts, axis=0) * scale_factor
    mixed_grad = jnp.concatenate(delta_parts, axis=1)
    position_grid = mixed_grad.reshape(seq_count, local_outer, inner_size, features)
    outer_rows = jnp.einsum(
        "pq,spjc->sqjc",
        outer_factor,
        lax.all_to_all(position_grid, "seq", split_axis=2, concat_axis=1, tiled=True),
        preferred_element_type=jnp.float32,
    )
    turned = (outer_rows * twiddle[None, :, :, None]).astype(jnp.bfloat16)
    turned_home = lax.all_to_all(turned, "seq", split_axis=1, concat_axis=2, tiled=True)
    back_term = jnp.einsum(
        "sipc,pj->sijc", turned_home, inner_factor, preferred_element_type=jnp.float32
    )
    back_term = lax.optimization_barrier(back_term.astype(jnp.bfloat16))
    input_grad = (position_grid.astype(jnp.float32) + back_term.astype(jnp.float32)).astype(
        jnp.bfloat16
    )
    input_grad = input_grad.reshape(seq_count, row_count, features)
    summed_in, summed_out = lax.psum((grad_in_local, grad_out_local), "seq")
    weight_in_grad, weight_out_grad = (
        lax.psum_scatter(summed_in, "dp", scatter_dimension=0, tiled=True),
        lax.psum_scatter(summed_out, "dp", scatter_dimension=0, tiled=True),
    )
    return (input_grad, weight_in_grad, weight_out_grad)


def solution(mesh):
    in_specs = (
        P("dp", "seq", None),
        P("dp", "seq", None),
        P("dp", None),
        P("dp", None),
        P("dp", None),
        P("dp", None),
        P(None, "seq"),
    )
    out_specs = (P("dp", "seq", None), P("dp", None), P("dp", None))
    return jax.shard_map(shards, mesh=mesh, in_specs=in_specs, out_specs=out_specs, check_vma=False)
```

profile of v0, /device:TPU:8, one launch (start us, length us, event | category | flops | bytes accessed | tf_op | source)
XLA Modules:
  0.0 514.5 jit_solution(14577318491672290920)
XLA Ops:
  7.2 19.0 %all_gather.13 = bf16[2048,128]{1,0:T(8,128)(2,1)S(1)} all-gather(bf16[256,128]{1,0:T(8,128)(2,1)} %param.9), channel_id=1, replica_groups=mesh['dp'=8,'seq'=32] {'dp'}, dimensions={0}, use_global_device_ids=true | all-gather | bytes 589824 | tf_op jit(solution)/shard_map/all_gather | solution.py:38
  26.1 3.7 fusion.25
  29.8 2.6 fusion.29
  32.5 2.7 fusion.33
  35.2 2.7 fusion.37
  37.9 15.3 %all_gather.12 = bf16[2048,128]{1,0:T(8,128)(2,1)S(1)} all-gather(bf16[256,128]{1,0:T(8,128)(2,1)S(1)} %copy-done.16), channel_id=1, replica_groups=mesh['dp'=8,'seq'=32] {'dp'}, dimensions={0}, use_global_device_ids=true | all-gather | bytes 589824 | tf_op jit(solution)/shard_map/all_gather | solution.py:39
  53.2 2.9 copy.23
  56.2 5.2 %multiply_convert_fusion.4 = bf16[2048,512]{1,0:T(8,128)(2,1)S(1)} fusion(f32[2048,512]{1,0:T(8,128)} %fusion.25, bf16[2048,512]{0,1:T(8,128)(2,1)S(1)} %bitcast.50, bf16[2048,128]{1,0:T(8,128)(2,1)S(1)} %all_gather.12), kind=kOutput, calls=%fused_computation.19 | convolution fusion | flops 287309824 | bytes 6946816 | tf_op jit(solution)/shard_map/dot_general | solution.py:29
  63.5 2.8 multiply_convert_fusion.5
  67.2 2.8 multiply_convert_fusion.6
  70.8 2.8 multiply_convert_fusion.7
  76.7 3.4 copy.25
  80.2 8.0 %all-to-all-start = ((bf16[1,8,256,512]{3,1,0,2:T(8,128)(2,1)}), bf16[1,8,256,512]{3,1,0,2:T(8,128)(2,1)}, u32[]{:S(2)}, u32[]{:S(2)}) async-start(bf16[1,8,256,512]{3,1,0,2:T(8,128)(2,1)} %copy.25), calls=%async_computation | async-start | bytes 4194304 | tf_op jit(solution)/shard_map/all_to_all | solution.py:75
  88.5 4.0 fusion.20
  99.8 23.0 %all_gather.14 = bf16[256,256]{1,0:T(8,128)(2,1)S(1)} all-gather(bf16[32,256]{1,0:T(8,128)(2,1)S(1)} %copy-done.17), channel_id=1, replica_groups=mesh['dp'=8,'seq'=32] {'dp'}, dimensions={0}, use_global_device_ids=true | all-gather | bytes 147456 | tf_op jit(solution)/shard_map/all_gather | solution.py:40
  125.3 3.0 fusion.8
  128.3 4.5 copy.29
  132.9 9.5 %all-to-all-start.1 = ((bf16[1,256,8,512]{3,2,0,1:T(8,128)(2,1)}), bf16[1,256,8,512]{3,2,0,1:T(8,128)(2,1)}, u32[]{:S(2)}, u32[]{:S(2)}) async-start(bf16[1,256,8,512]{3,2,0,1:T(8,128)(2,1)} %copy.29), calls=%async_computation.1 | async-start | bytes 4194304 | tf_op jit(solution)/shard_map/all_to_all | solution.py:79
  142.7 2.6 fusion.23
  145.3 2.5 fusion.27
  150.5 28.9 %all_gather.15 = bf16[256,256]{1,0:T(8,128)(2,1)S(1)} all-gather(bf16[32,256]{1,0:T(8,128)(2,1)S(1)} %copy-done.18), channel_id=1, replica_groups=mesh['dp'=8,'seq'=32] {'dp'}, dimensions={0}, use_global_device_ids=true | all-gather | bytes 147456 | tf_op jit(solution)/shard_map/all_gather | solution.py:41
  179.4 11.2 %reduce-scatter.3.cloned.1.call-done = f32[256,128]{1,0:T(8,128)} async-done(((f32[2048,128]{1,0:T(8,128)}), f32[256,128]{1,0:T(8,128)}) %reduce-scatter.3.cloned.1.call-update) | async-done | bytes 131088 | tf_op jit(solution)/shard_map/reduce_scatter | solution.py:90
  195.0 3.9 copy.32
  198.9 306.0 %all-reduce.3.cloned.1.call-done = (f32[256,128]{1,0:T(8,128)}, f32[256,128]{1,0:T(8,128)}) async-done(((f32[256,128]{1,0:T(8,128)}, f32[256,128]{1,0:T(8,128)}), (f32[256,128]{1,0:T(8,128)}, f32[256,128]{1,0:T(8,128)})) %all-reduce.3.cloned.1.call-update) | async-done | bytes 262160 | tf_op jit(solution)/shard_map/psum | solution.py:88
  (68 shorter events, 27.2 us)
Async XLA Ops:
  7.2 22.7 %copy-start.8 = (bf16[1,2048,512]{2,1,0:T(8,128)(2,1)S(1)}, bf16[1,2048,512]{2,1,0:T(8,128)(2,1)}, u32[]{:S(2)}) copy-start(bf16[1,2048,512]{2,1,0:T(8,128)(2,1)} %param.7) | copy-start | bytes 6291460
  32.5 5.4 %copy-start.16 = (bf16[256,128]{1,0:T(8,128)(2,1)S(1)}, bf16[256,128]{1,0:T(8,128)(2,1)}, u32[]{:S(2)}) copy-start(bf16[256,128]{1,0:T(8,128)(2,1)} %param.10) | copy-start | bytes 196612
  56.1 17.5 %copy-start = (bf16[1,2048,512]{1,2,0:T(8,128)(2,1)}, bf16[1,2048,512]{1,2,0:T(8,128)(2,1)S(1)}, u32[]{:S(2)}) copy-start(bf16[1,2048,512]{1,2,0:T(8,128)(2,1)S(1)} %copy.23) | copy-start | bytes 6291460
  56.2 7.4 %copy-start.6 = (f32[2048,512]{1,0:T(8,128)S(1)}, f32[2048,512]{1,0:T(8,128)}, u32[]{:S(2)}) copy-start(f32[2048,512]{1,0:T(8,128)} %fusion.29) | copy-start | bytes 12582916
  63.5 3.7 copy-start.4
  66.3 3.7 copy-start.11
  67.2 3.7 copy-start.2
  70.0 3.7 copy-start.12
  73.7 1.4 copy-start.14
  80.2 42.6 %all-to-all-start = ((bf16[1,8,256,512]{3,1,0,2:T(8,128)(2,1)}), bf16[1,8,256,512]{3,1,0,2:T(8,128)(2,1)}, u32[]{:S(2)}, u32[]{:S(2)}) async-start(bf16[1,8,256,512]{3,1,0,2:T(8,128)(2,1)} %copy.25), calls=%async_computation | async-start | bytes 4194304 | tf_op jit(solution)/shard_map/all_to_all | solution.py:75
  88.2 91.2 %reduce-scatter.5.cloned.1.call-start = ((), (), s32[]{:S(2)}) async-start(), calls=%async_computation.5 | async-start | bytes 1179648 | tf_op jit(solution)/shard_map/reduce_scatter | solution.py:91
  88.5 4.0 copy-start.1
  88.5 4.2 copy-start.7
  92.7 2.2 copy-start.5
  94.9 2.2 copy-start.3
  97.1 2.7 copy-start.17
  122.8 2.6 copy-start.19
  132.9 57.8 %all-to-all-start.1 = ((bf16[1,256,8,512]{3,2,0,1:T(8,128)(2,1)}), bf16[1,256,8,512]{3,2,0,1:T(8,128)(2,1)}, u32[]{:S(2)}, u32[]{:S(2)}) async-start(bf16[1,256,8,512]{3,2,0,1:T(8,128)(2,1)} %copy.29), calls=%async_computation.1 | async-start | bytes 4194304 | tf_op jit(solution)/shard_map/all_to_all | solution.py:79
  142.4 48.3 %reduce-scatter.3.cloned.1.call-start = ((), (), s32[]{:S(2)}) async-start(), calls=%async_computation.4 | async-start | bytes 1179648 | tf_op jit(solution)/shard_map/reduce_scatter | solution.py:90
  142.7 5.1 copy-start.9
  142.7 5.1 copy-start.13
  142.7 5.8 %copy-start.15 = (bf16[2048,512]{1,0:T(8,128)(2,1)S(1)}, bf16[2048,512]{1,0:T(8,128)(2,1)}, u32[]{:S(2)}) copy-start(bf16[2048,512]{1,0:T(8,128)(2,1)} %copy-done.14) | copy-start | bytes 6291460
  147.8 2.7 copy-start.18
  150.4 354.5 %all-reduce.3.cloned.1.call-start = ((), (), s32[]{:S(2)}) async-start(), calls=%async_computation.6 | async-start | bytes 524288 | tf_op jit(solution)/shard_map/psum | solution.py:88
  (1 other events, 1.3 us)
Sparse Core Ops, SparseCore 0:
  99.9 39.1 reduce-scatter.4
  150.5 40.0 reduce-scatter.2
  193.3 311.5 all-reduce.2
where the time goes:
time: 515 us
  waiting for transfers between devices  317 us (62%)
  blocking collectives  86.2 us (17%)
  matrix products  49.1 us (10%)
  local copies, waits for them, and re-layouts  25.5 us (5%)
  starting transfers between devices  18.1 us (4%)
  between operations  14.1 us (3%)
    psum x1, waiting for transfers between devices, shards(): summed_in, summed_out = lax.psum((grad_in_local, grad_out_local), 'seq')  306 us
    all_gather x1, blocking collectives, shards(): lax.all_gather(inner_factor, 'dp', axis=0, tiled=True)  28.9 us
    dot_general x8, matrix products, width_product(): lax.dot_general(left_rows, right_rows, (((1,), (1,)), ((), ())), preferre...  25.3 us
    all_gather x1, blocking collectives, shards(): lax.all_gather(outer_factor, 'dp', axis=0, tiled=True)  23 us
    all_gather x1, blocking collectives, shards(): lax.all_gather(weight_in, 'dp', axis=0, tiled=True)  19 us
    all_gather x1, blocking collectives, shards(): lax.all_gather(weight_out, 'dp', axis=0, tiled=True)  15.3 us
    dot_general x8, matrix products, token_product(): lax.dot_general(left_rows, right_rows, (((0,), (0,)), ((), ())), preferre...  15.1 us
    reduce_scatter x1, waiting for transfers between devices, shards(): lax.psum_scatter(summed_in, 'dp', scatter_dimension=0, tiled=True)  11.2 us
  transfers between devices with their start and end apart: 5, of which 2 were waited for; matrix products, arithmetic and copies ran while one was open for 7% of the time, Pallas kernels for 0%

commit v1 on v0

v1 whole, which is shorter than its diff:
```python
import math

import jax
import jax.numpy as jnp
from jax import lax
from jax.experimental import pallas as pl
from jax.experimental.pallas import tpu as pltpu
from jax.sharding import PartitionSpec as P


NB = 4
BF = jnp.bfloat16
F32 = jnp.float32
CUBIC = 0.044715


def gelu_parts(pre_act):
    coeff = math.sqrt(2.0 / math.pi)
    squared = pre_act * pre_act
    tangent = jnp.tanh(pre_act * (coeff + (coeff * CUBIC) * squared))
    half = 0.5 * tangent + 0.5
    activated = pre_act * half
    slope = half + activated * (1.0 - half) * (2.0 * coeff + (6.0 * coeff * CUBIC) * squared)
    return activated, slope


def width_product(left_rows, right_rows):
    return lax.dot_general(
        left_rows, right_rows, (((1,), (1,)), ((), ())), preferred_element_type=F32
    )


def token_product(left_rows, right_rows):
    return lax.dot_general(
        left_rows, right_rows, (((0,), (0,)), ((), ())), preferred_element_type=F32
    )


def pack_kernel(in_ref, out_ref, outer_ref, inner_ref, pack_ref):
    half_hidden, width = in_ref.shape
    rows = outer_ref.shape[0]
    pack_ref[:half_hidden] = in_ref[...]
    pack_ref[half_hidden : 2 * half_hidden] = out_ref[...]
    start = 2 * half_hidden
    for ref in (outer_ref, inner_ref):
        for n in range(2):
            pack_ref[start : start + rows] = ref[:, n * width : (n + 1) * width]
            start += rows


def pack_shards(weight_in, weight_out, outer_factor, inner_factor):
    half_hidden, width = weight_in.shape
    rows = 2 * half_hidden + 4 * outer_factor.shape[0]
    vmem = pl.BlockSpec(memory_space=pltpu.VMEM)
    return pl.pallas_call(
        pack_kernel,
        out_shape=jax.ShapeDtypeStruct((rows, width), BF),
        in_specs=[vmem] * 4,
        out_specs=vmem,
        name="pack",
    )(weight_in, weight_out, outer_factor, inner_factor)


def block_kernel(steps, sub, half_hidden, *refs):
    saved_ref, up_ref = refs[1:3]
    pieces = refs[3 : 3 + 2 * steps]
    chunk_ref, keep_ref, send_ref, weight_ref, acc_ref = refs[3 + 2 * steps :]
    step = pl.program_id(0)
    for n in range(steps):

        @pl.when(step == n)
        def _(n=n):
            for side in range(2):
                weight_ref[side] = pieces[2 * n + side][: 2 * half_hidden]

    groups = chunk_ref.shape[0]
    inner = sub // groups
    tiles = saved_ref.shape[0] // sub
    width = saved_ref.shape[1]

    def weights(side):
        return weight_ref[side, :half_hidden], weight_ref[side, half_hidden:]

    def first(t):
        saved = saved_ref[t * sub : (t + 1) * sub]
        up = up_ref[t * sub : (t + 1) * sub]
        return (
            saved,
            up,
            [
                (width_product(saved, weights(side)[0]), width_product(up, weights(side)[1]))
                for side in range(2)
            ],
        )

    def second(t, state):
        saved, up, products = state
        total = up.astype(F32)
        for side, (pre_act, act_grad) in enumerate(products):
            activated, slope = gelu_parts(pre_act)
            pre_grad = (act_grad * slope).astype(BF)
            total += jnp.dot(pre_grad, weights(side)[0], preferred_element_type=F32)
            sums = (
                token_product(saved, pre_grad),
                token_product(up, activated.astype(BF)),
            )
            for which, value in enumerate(sums):
                if t == 0:
                    acc_ref[2 * side + which] = value
                else:
                    acc_ref[2 * side + which] += value
        chunk_ref[:, t * inner : (t + 1) * inner, :] = total.reshape(groups, inner, width).astype(
            BF
        )

    state = first(0)
    for t in range(tiles):
        ahead = first(t + 1) if t + 1 < tiles else None
        second(t, state)
        state = ahead
    for which in range(2):
        keep_ref[0, which] = acc_ref[which].T
        send_ref[0, which] = acc_ref[2 + which].T


def block_steps(block_ids, saved, up, pieces, groups, inner_size, total_rows, base, carried):
    steps = len(pieces) // 2
    tokens, features = saved.shape
    width = features // NB
    half_hidden = pieces[0].shape[0] // 5 * 2
    per_block = tokens // groups
    out_shape = (
        jax.ShapeDtypeStruct((groups, total_rows, width), BF),
        jax.ShapeDtypeStruct((steps, 2, half_hidden, width), F32),
        jax.ShapeDtypeStruct((steps, 2, half_hidden, width), F32),
    )
    piece = pl.BlockSpec(pieces[0].shape, lambda n, b: (0, 0))
    token_spec = pl.BlockSpec((tokens, width), lambda n, b: (0, b[n]))
    grad_spec = pl.BlockSpec((1, 2, half_hidden, width), lambda n, b: (n, 0, 0, 0))
    extra = [] if carried is None else [carried]

    def body(*refs):
        used = 3 + 2 * steps
        block_kernel(steps, inner_size, half_hidden, *refs[:used], *refs[used + len(extra) :])

    return pl.pallas_call(
        body,
        out_shape=out_shape,
        grid_spec=pltpu.PrefetchScalarGridSpec(
            num_scalar_prefetch=1,
            grid=(steps,),
            in_specs=[token_spec, token_spec]
            + [piece] * (2 * steps)
            + [pl.BlockSpec(memory_space=pl.ANY)] * len(extra),
            out_specs=(
                pl.BlockSpec((groups, per_block, width), lambda n, b: (0, n + base, 0)),
                grad_spec,
                grad_spec,
            ),
            scratch_shapes=[
                pltpu.VMEM((2, 2 * half_hidden, width), BF),
                pltpu.VMEM((4, width, half_hidden), F32),
            ],
        ),
        input_output_aliases={3 + 2 * steps: 0} if extra else {},
    )(block_ids, saved, up, *pieces, *extra)


def factor_kernel(rows_ref, *refs):
    pieces = refs[:8]
    outer_ref, inner_ref, outer_scr, inner_scr = refs[8:]
    lanes = pieces[0].shape[1]
    for n, piece in enumerate(pieces):
        rows = 32
        start = pl.ds(pl.multiple_of(rows_ref[n], rows), rows)
        base = piece.shape[0] - 4 * rows
        for k, scr in enumerate((outer_scr, outer_scr, inner_scr, inner_scr)):
            col = (k % 2) * lanes
            scr[start, col : col + lanes] = piece[
                base + k * rows : base + (k + 1) * rows
            ].astype(F32)
    outer_ref[...] = outer_scr[...].T.astype(BF)
    inner_ref[...] = inner_scr[...].T.astype(BF)


def assemble_factors(row_starts, pieces, size):
    full = jax.ShapeDtypeStruct((size, size), BF)
    vmem = pl.BlockSpec(memory_space=pltpu.VMEM)
    return pl.pallas_call(
        factor_kernel,
        out_shape=(full, full),
        in_specs=[pl.BlockSpec(memory_space=pltpu.SMEM)] + [vmem] * 8,
        out_specs=(vmem, vmem),
        scratch_shapes=[pltpu.VMEM((size, size), F32)] * 2,
        name="factors",
    )(row_starts, *pieces)


def outer_kernel(recv_ref, factor_ref, twiddle_ref, *refs):
    out_ref, rows_ref = refs[-2:]
    groups, per_block, width = recv_ref.shape
    inner = twiddle_ref.shape[1]
    size = factor_ref.shape[0]
    rows_ref[...] = recv_ref[...].reshape(groups * per_block, width).astype(F32)
    for j in range(0, inner, 2):
        pair = jnp.concatenate(
            [rows_ref[pl.ds(j + n, size, inner), :] for n in range(2)], axis=1
        ).astype(BF)
        mixed = jnp.dot(factor_ref[...], pair, preferred_element_type=F32)
        parts = [
            (mixed[:, n * width : (n + 1) * width] * twiddle_ref[:, j + n : j + n + 1]).reshape(
                groups, size // groups, width
            )
            for n in range(2)
        ]
        step = size // groups
        out_ref[:, j * step : (j + 2) * step, :] = jnp.concatenate(parts, axis=1).astype(BF)


def outer_mix(recv, factor_t, twiddle, per_block, steps, total_rows):
    groups, _, width = recv.shape
    return pl.pallas_call(
        outer_kernel,
        out_shape=jax.ShapeDtypeStruct((groups, total_rows, width), BF),
        grid=(steps,),
        in_specs=[
            pl.BlockSpec((groups, per_block, width), lambda b: (0, b, 0)),
            pl.BlockSpec(factor_t.shape, lambda b: (0, 0)),
            pl.BlockSpec(twiddle.shape, lambda b: (0, 0)),
        ],
        out_specs=pl.BlockSpec((groups, per_block, width), lambda b: (0, b, 0)),
        scratch_shapes=[pltpu.VMEM((groups * per_block, width), F32)],
    )(recv, factor_t, twiddle)


def pair_add_kernel(*refs):
    out_ref = refs[-1]
    groups = out_ref.shape[0]
    halves = (len(refs) - 1) // 2
    row = 0
    for keep_ref, got_ref in zip(refs[:halves], refs[halves : 2 * halves]):
        rows = keep_ref.shape[2] // groups
        for step in range(keep_ref.shape[0]):
            parts = [
                (keep_ref[step, which] + got_ref[step, which]).reshape(groups, rows, -1)
                for which in range(2)
            ]
            out_ref[:, row : row + 2 * rows, :] = jnp.concatenate(parts, axis=1).astype(BF)
            row += 2 * rows


def put_pair_sums(keeps, gots, groups, total_rows, start, carried):
    half_hidden, width = keeps[0].shape[2:]
    rows = sum(keep.shape[0] for keep in keeps) * 2 * (half_hidden // groups)
    arrays = [*keeps, *gots]
    extra = [] if carried is None else [carried]

    def body(*refs):
        pair_add_kernel(*refs[: len(arrays)], refs[-1])

    return pl.pallas_call(
        body,
        out_shape=jax.ShapeDtypeStruct((groups, total_rows, width), BF),
        grid=(1,),
        in_specs=[pl.BlockSpec(x.shape, lambda n: (0, 0, 0, 0)) for x in arrays]
        + [pl.BlockSpec(memory_space=pl.ANY)] * len(extra),
        out_specs=pl.BlockSpec((groups, rows, width), lambda n: (0, start // rows, 0)),
        input_output_aliases={len(arrays): 0} if extra else {},
    )(*arrays, *extra)


def seq_sum_kernel(parts_ref, *out_refs):
    total = jnp.sum(parts_ref[...].astype(F32), axis=0)
    rows = out_refs[0].shape[0]
    for n, ref in enumerate(out_refs):
        ref[...] = total[n * rows : (n + 1) * rows]


def seq_sums(recv, rows, count):
    groups, all_rows, width = recv.shape
    part = (rows // count, width)
    return pl.pallas_call(
        seq_sum_kernel,
        out_shape=[jax.ShapeDtypeStruct(part, F32)] * count,
        grid=(1,),
        in_specs=[pl.BlockSpec((groups, rows, width), lambda n: (0, all_rows // rows - 1, 0))],
        out_specs=[pl.BlockSpec(part, lambda n: (0, 0))] * count,
    )(recv)


def spread_kernel(scale, *refs):
    out_ref = refs[-1]
    total = refs[0][...]
    for ref in refs[1:-2]:
        total += ref[...]
    out_ref[...] = jnp.broadcast_to((total * scale)[None], out_ref.shape).astype(BF)


def spread_rows(parts, buffer, scale):
    groups, all_rows, width = buffer.shape
    rows = parts[0].shape[0]
    return pl.pallas_call(
        lambda *refs: spread_kernel(scale, *refs),
        out_shape=jax.ShapeDtypeStruct(buffer.shape, BF),
        grid=(1,),
        in_specs=[pl.BlockSpec(x.shape, lambda n: (0, 0)) for x in parts]
        + [pl.BlockSpec(memory_space=pl.ANY)],
        out_specs=pl.BlockSpec((groups, rows, width), lambda n: (0, all_rows // rows - 1, 0)),
        input_output_aliases={len(parts): 0},
    )(*parts, buffer)


def inner_kernel(has_rows, ids_ref, recv_ref, mixed_ref, factor_ref, *refs):
    rows_ref = refs[-1]
    out_ref = refs[-4] if has_rows else refs[-2]
    groups, per_block, width = recv_ref.shape
    size = factor_ref.shape[0]
    inner = size // groups
    outer = per_block // inner
    rows_ref[...] = recv_ref[...].reshape(groups * per_block, width).astype(F32)
    for i in range(0, outer, 2):
        pair = jnp.concatenate(
            [rows_ref[pl.ds(i + n, size, outer), :] for n in range(2)], axis=1
        ).astype(BF)
        back = jnp.dot(factor_ref[...], pair, preferred_element_type=F32)
        back = back.astype(BF).astype(F32)
        residual = mixed_ref[:, i * inner : (i + 2) * inner, :].astype(F32)
        for n in range(2):
            own = residual[:, n * inner : (n + 1) * inner, :].reshape(size, width)
            out_ref[(i + n) * size : (i + n + 1) * size, :] = (
                own + back[:, n * width : (n + 1) * width]
            ).astype(BF)
    if has_rows:
        grads = refs[0][...].astype(F32)
        rows = grads.shape[1] // 2
        for which in range(2):
            part = grads[:, which * rows : (which + 1) * rows]
            refs[-3 + which][...] = part.reshape(groups * rows, width)


def inner_mix(block_ids, recv, mixed, factor_t, carried, per_block, grad_rows):
    groups, all_rows, width = recv.shape
    steps = block_ids.shape[0]
    spec = pl.BlockSpec((groups, per_block, width), lambda n, b: (0, n, 0))
    tokens = groups * per_block
    has_rows = carried is not None
    extra = [recv, carried] if has_rows else []
    out_shape = [jax.ShapeDtypeStruct((tokens, NB * width), BF)]
    out_specs = [pl.BlockSpec((tokens, width), lambda n, b: (0, b[n]))]
    extra_specs = []
    if has_rows:
        extra_specs = [
            pl.BlockSpec(
                (groups, grad_rows, width), lambda n, b: (0, all_rows // grad_rows - 1, 0)
            ),
            pl.BlockSpec(memory_space=pl.ANY),
        ]
        full = (groups * grad_rows // 2, width)
        out_shape += [jax.ShapeDtypeStruct(full, F32)] * 2
        out_specs += [pl.BlockSpec(full, lambda n, b: (0, 0))] * 2
    return pl.pallas_call(
        lambda *refs: inner_kernel(has_rows, *refs),
        out_shape=out_shape,
        grid_spec=pltpu.PrefetchScalarGridSpec(
            num_scalar_prefetch=1,
            grid=(steps,),
            in_specs=[spec, spec, pl.BlockSpec(factor_t.shape, lambda n, b: (0, 0))] + extra_specs,
            out_specs=out_specs,
            scratch_shapes=[pltpu.VMEM((tokens, width), F32)],
        ),
        input_output_aliases={5: 0} if has_rows else {},
    )(block_ids, recv, mixed, factor_t, *extra)


def shards(saved_mixed, out_grad, weight_in, weight_out, outer_factor, inner_factor, twiddle):
    data_devices = lax.axis_size("dp")
    seq_devices = lax.axis_size("seq")
    seq_count, row_count, features = saved_mixed.shape
    inner_size = inner_factor.shape[1]
    scale_factor = 1.0 / math.sqrt(seq_count * data_devices * row_count * seq_devices)
    tokens = seq_count * row_count
    saved = saved_mixed.reshape(tokens, features)
    upstream = out_grad.reshape(tokens, features)

    dp_index = lax.axis_index("dp")
    chip = dp_index // 2
    core = dp_index % 2
    per_block = tokens // seq_devices

    def swap(piece):
        pairs = [(i, i ^ 1) for i in range(data_devices)]
        return lax.ppermute(piece, "dp", pairs)

    def from_chip(piece, step):
        pairs = [((i + 2 * step) % data_devices, i) for i in range(data_devices)]
        return lax.ppermute(piece, "dp", pairs)

    def exchange(array):
        return lax.all_to_all(array, "seq", split_axis=0, concat_axis=0, tiled=True)

    offsets = (0, 1, 3, 2)
    ids = jnp.stack([(chip + offset) % NB for offset in offsets]).astype(jnp.int32)
    pack = pack_shards(weight_in, weight_out, outer_factor, inner_factor)
    near = [pack]
    for n in range(1, NB):
        near.append(from_chip(pack, offsets[n]))
    far = []
    for n in range(NB):
        far.append(swap(near[n]))
    half_hidden = weight_in.shape[0]
    grad_rows = 2 * half_hidden // seq_devices
    half_rows = (NB // 2) * per_block
    rows_of = (half_rows, half_rows + NB * grad_rows)
    calls = ((0, 1, 0, 0), (1, 2, 0, 1), (2, 4, 1, 0))
    chunks = [None, None]
    keeps = []
    gots = []
    for n, (begin, end, target, base) in enumerate(calls):
        pieces = [side[step] for step in range(begin, end) for side in (near, far)]
        chunks[target], keep, send = block_steps(
            ids[begin:end],
            saved,
            upstream,
            pieces,
            seq_devices,
            inner_size,
            rows_of[target],
            base,
            chunks[target],
        )
        keeps.append(keep)
        gots.append(swap(send))
        if n > 0:
            group = slice(0, 2) if n == 1 else slice(2, 3)
            start = half_rows + (n - 1) * 2 * grad_rows
            chunks[1] = put_pair_sums(
                keeps[group], gots[group], seq_devices, rows_of[1], start, chunks[1]
            )

    factor_rows = outer_factor.shape[0]
    starts = jnp.concatenate([2 * ids + core, 2 * ids + 1 - core]).astype(jnp.int32) * factor_rows
    outer_t, inner_t = assemble_factors(starts, near + far, inner_size)
    buffers = []
    for half in range(2):
        arrived = exchange(chunks[half])
        buffers.append(
            outer_mix(arrived, outer_t, twiddle, per_block, NB // 2, half_rows + half * grad_rows)
        )
    sums = seq_sums(arrived, NB * grad_rows, NB)
    parts = [sums[0]]
    for n in range(1, NB):
        parts.append(from_chip(sums[n], -offsets[n]))
    home = [exchange(buffers[0])]
    second = spread_rows(parts, buffers[1], scale_factor)
    home.append(exchange(second))
    carried = None
    for half in range(2):
        outs = inner_mix(
            ids[2 * half : 2 * half + 2],
            home[half],
            chunks[half],
            inner_t,
            carried,
            per_block,
            grad_rows,
        )
        carried = outs[0]
    input_grad = carried.reshape(seq_count, row_count, features)
    return (input_grad, outs[1], outs[2])


def solution(mesh):
    in_specs = (
        P("dp", "seq", None),
        P("dp", "seq", None),
        P("dp", None),
        P("dp", None),
        P("dp", None),
        P("dp", None),
        P(None, "seq"),
    )
    out_specs = (P("dp", "seq", None), P("dp", None), P("dp", None))
    return jax.shard_map(shards, mesh=mesh, in_specs=in_specs, out_specs=out_specs, check_vma=False)
```

time: 515 us -> 166 us (0.32)
  waiting for transfers between devices: 317 us -> 61.9 us
  blocking collectives: 86.2 us -> 0 us
  matrix products: 49.1 us -> 0 us
  Pallas kernels: 0 us -> 44.8 us
  starting transfers between devices: 18.1 us -> 48.3 us
  local copies, waits for them, and re-layouts: 25.5 us -> 7.68 us
  between operations: 14.1 us -> 0.78 us
    psum x1 -> x0, waiting for transfers between devices: 306 us -> none  [shards(): summed_in, summed_out = lax.psum((grad_in_local, grad_out_local), 'seq')]
    all_gather x4 -> x0, blocking collectives: 86.2 us -> none  [the longest x1 28.9 us: shards(): lax.all_gather(inner_factor, 'dp', axis=0, tiled=True)]
    dot_general x22 -> x0, matrix products: 49.1 us -> none  [the longest x8 25.3 us: width_product(): lax.dot_general(left_rows, right_rows, (((1,), (1,)), ((), ())), preferre...]
    pallas_call x0 -> x13, Pallas kernels: none -> 44.8 us  [the longest x3 20.9 us: block_steps(): pl.pallas_call(body, out_shape=out_shape, grid_spec=pltpu.PrefetchScalarG...]
    ppermute x0 -> x13, waiting for transfers between devices: none -> 35.9 us  [the longest x6 34.1 us: from_chip(): return lax.ppermute(piece, 'dp', pairs)]
    all_to_all x2 -> x4, waiting for transfers between devices: 0.01 us -> 26 us  [exchange(): return lax.all_to_all(array, 'seq', split_axis=0, concat_axis=0, tiled=True)]
    ppermute x0 -> x13, starting transfers between devices: none -> 19.5 us  [the longest x6 18.5 us: from_chip(): return lax.ppermute(piece, 'dp', pairs)]
    all_to_all x2 -> x4, starting transfers between devices: 17.5 us -> 28.8 us  [exchange(): return lax.all_to_all(array, 'seq', split_axis=0, concat_axis=0, tiled=True)]
  transfers between devices with their start and end apart: 5 -> 17, of which waited for: 2 -> 8; matrix products, arithmetic and copies ran while one was open for 7% -> 2% of each run, Pallas kernels for 0% -> 21%
where the time goes in v1:
time: 166 us; the launch traced here: 165 us
  waiting for transfers between devices  61.9 us (37%)
  starting transfers between devices  48.3 us (29%)
  Pallas kernels  44.8 us (27%)
  local copies, waits for them, and re-layouts  7.68 us (5%)
  other arithmetic  1.84 us (1%)
    ppermute x6, waiting for transfers between devices, from_chip(): return lax.ppermute(piece, 'dp', pairs)  34.1 us
    all_to_all x4, starting transfers between devices, exchange(): return lax.all_to_all(array, 'seq', split_axis=0, concat_axis=0, tiled=True)  28.8 us
    all_to_all x4, waiting for transfers between devices, exchange(): return lax.all_to_all(array, 'seq', split_axis=0, concat_axis=0, tiled=True)  26 us
    pallas_call x3, Pallas kernels, block_steps(): pl.pallas_call(body, out_shape=out_shape, grid_spec=pltpu.PrefetchScalarG...  20.9 us
    ppermute x6, starting transfers between devices, from_chip(): return lax.ppermute(piece, 'dp', pairs)  18.5 us
    unnamed x43, local copies, waits for them, and re-layouts  7.68 us
    pallas_call x2, Pallas kernels, inner_mix(): pl.pallas_call(lambda *refs: inner_kernel(has_rows, *refs), out_shape=out...  7.23 us
    pallas_call x2, Pallas kernels, outer_mix(): pl.pallas_call(outer_kernel, out_shape=jax.ShapeDtypeStruct((groups, tota...  5.85 us
  transfers between devices with their start and end apart: 17, of which 8 were waited for; matrix products, arithmetic and copies ran while one was open for 2% of the time, Pallas kernels for 21%

profile of v1, /device:TPU:8, one launch (start us, length us, event | category | flops | bytes accessed | tf_op | source)
XLA Modules:
  0.0 165.4 jit_solution(5986906335502076702)
XLA Ops:
  2.2 6.3 %collective-permute-start.5 = (bf16[640,128]{1,0:T(8,128)(2,1)}, bf16[640,128]{1,0:T(8,128)(2,1)S(1)}, u32[]{:S(2)}, u32[]{:S(2)}) collective-permute-start(bf16[640,128]{1,0:T(8,128)(2,1)} %pack.1.refs_3_.refs_0_), channel_id=1, source_target_pairs={{64,0},{96,32},{128,64},{160,96},{192,128},{224,160},{0,192},{32,2... | collective-permute-start | bytes 491528 | tf_op jit(solution)/shard_map/ppermute | solution.py:396
  8.5 7.3 %collective-permute-done.5.refs_3_.refs_1_ = bf16[640,128]{1,0:T(8,128)(2,1)S(1)} collective-permute-done((bf16[640,128]{1,0:T(8,128)(2,1)}, bf16[640,128]{1,0:T(8,128)(2,1)S(1)}, u32[]{:S(2)}, u32[]{:S(2)}) %collective-permute-start.5) | collective-permute-done | bytes 163872 | tf_op jit(solution)/shard_map/ppermute | solution.py:396
  16.5 5.6 %shard_map.94 = (bf16[32,128,128]{2,1,0:T(8,128)(2,1)}, f32[1,2,256,128]{3,2,1,0:T(8,128)}, f32[1,2,256,128]{3,2,1,0:T(8,128)}) custom-call(s32[1]{0:T(128)} %bitcast.4.refs_0_, bf16[2048,512]{1,0:T(8,128)(2,1)} %bitcast.7, bf16[2048,512]{1,0:T(8,128)(2,1)} %bitcast.10, bf16[640,128]{1,0:T(8,128)(2,1)} %pack.1.refs_3_.refs_0_, bf16[640,128]{1,0:T(8,128)(2,1)} %copy-done.6), custom_call_target="tpu_custom_call" | custom-call | tf_op jit(solution)/shard_map/pallas_call | solution.py:146
  22.7 5.6 %shard_map.95 = (bf16[32,128,128]{2,1,0:T(8,128)(2,1)}, f32[1,2,256,128]{3,2,1,0:T(8,128)}, f32[1,2,256,128]{3,2,1,0:T(8,128)}) custom-call(s32[1]{0:T(128)} %bitcast.5.refs_0_, bf16[2048,512]{1,0:T(8,128)(2,1)} %bitcast.8, bf16[2048,512]{1,0:T(8,128)(2,1)} %bitcast.11, bf16[640,128]{1,0:T(8,128)(2,1)} %copy-done.5, ...), custom_call_target="tpu_custom_call", output_to_operand_aliasing={{0}: (5, {})} | custom-call | tf_op jit(solution)/shard_map/pallas_call | solution.py:146
  28.4 7.7 %all-to-all-start.2 = ((bf16[32,128,128]{2,1,0:T(8,128)(2,1)}), bf16[32,128,128]{2,1,0:T(8,128)(2,1)S(1)}, u32[]{:S(2)}, u32[]{:S(2)}) async-start(bf16[32,128,128]{2,1,0:T(8,128)(2,1)} %get-tuple-element.35.refs_2_), calls=%async_computation.2 | async-start | bytes 2097152 | tf_op jit(solution)/shard_map/all_to_all | solution.py:399
  36.0 4.2 %collective-permute-start.2 = (bf16[640,128]{1,0:T(8,128)(2,1)S(1)}, bf16[640,128]{1,0:T(8,128)(2,1)S(1)}, u32[]{:S(2)}, u32[]{:S(2)}) collective-permute-start(bf16[640,128]{1,0:T(8,128)(2,1)S(1)} %copy-done.4), channel_id=1, source_target_pairs={{128,0},{160,32},{192,64},{224,96},{0,128},{32,160},{64,192},{96,2... | collective-permute-start | bytes 491528 | tf_op jit(solution)/shard_map/ppermute | solution.py:396
  40.3 2.7 %collective-permute-start = (bf16[640,128]{1,0:T(8,128)(2,1)S(1)}, bf16[640,128]{1,0:T(8,128)(2,1)S(1)}, u32[]{:S(2)}, u32[]{:S(2)}) collective-permute-start(bf16[640,128]{1,0:T(8,128)(2,1)S(1)} %copy-done.4), channel_id=1, source_target_pairs={{192,0},{224,32},{0,64},{32,96},{64,128},{96,160},{128,192},{160,2... | collective-permute-start | bytes 491528 | tf_op jit(solution)/shard_map/ppermute | solution.py:396
  43.5 17.8 %collective-permute-done.2.refs_5_.refs_3_ = bf16[640,128]{1,0:T(8,128)(2,1)S(1)} collective-permute-done((bf16[640,128]{1,0:T(8,128)(2,1)S(1)}, bf16[640,128]{1,0:T(8,128)(2,1)S(1)}, u32[]{:S(2)}, u32[]{:S(2)}) %collective-permute-start.2) | collective-permute-done | bytes 163872 | tf_op jit(solution)/shard_map/ppermute | solution.py:396
  61.3 5.3 %collective-permute-done.refs_3_.refs_2_ = bf16[640,128]{1,0:T(8,128)(2,1)S(1)} collective-permute-done((bf16[640,128]{1,0:T(8,128)(2,1)S(1)}, bf16[640,128]{1,0:T(8,128)(2,1)S(1)}, u32[]{:S(2)}, u32[]{:S(2)}) %collective-permute-start) | collective-permute-done | bytes 163872 | tf_op jit(solution)/shard_map/ppermute | solution.py:396
  68.0 2.0 %shard_map.96.refs_7_ = bf16[32,192,128]{2,1,0:T(8,128)(2,1)} custom-call(f32[1,2,256,128]{3,2,1,0:T(8,128)} %get-tuple-element.21.refs_0_, f32[1,2,256,128]{3,2,1,0:T(8,128)} %get-tuple-element.23.refs_1_, f32[1,2,256,128]{3,2,1,0:T(8,128)} %copy-done.13, f32[1,2,256,128]{3,2,1,0:T(8,128)} %copy-done.14), custom_call_target="tpu_custom_call" | custom-call | tf_op jit(solution)/shard_map/pallas_call | solution.py:261
  71.4 9.7 %shard_map.97 = (bf16[32,192,128]{2,1,0:T(8,128)(2,1)}, f32[2,2,256,128]{3,2,1,0:T(8,128)}, f32[2,2,256,128]{3,2,1,0:T(8,128)}) custom-call(s32[2]{0:T(128)} %pad_add_fusion.refs_0_, bf16[2048,512]{1,0:T(8,128)(2,1)} %bitcast.9, bf16[2048,512]{1,0:T(8,128)(2,1)} %bitcast.12, bf16[640,128]{1,0:T(8,128)(2,1)} %copy-done.9, ...), custom_call_target="tpu_custom_call", output_to_operand_aliasing={{0}: (7, {})} | custom-call | tf_op jit(solution)/shard_map/pallas_call | solution.py:146
  84.1 2.0 %shard_map.98.refs_2_ = bf16[32,192,128]{2,1,0:T(8,128)(2,1)} custom-call(f32[2,2,256,128]{3,2,1,0:T(8,128)} %get-tuple-element.26.refs_0_, f32[2,2,256,128]{3,2,1,0:T(8,128)} %copy-done.12, bf16[32,192,128]{2,1,0:T(8,128)(2,1)} %get-tuple-element.28.refs_2_), custom_call_target="tpu_custom_call", output_to_operand_aliasing={{}: (2, {})} | custom-call | tf_op jit(solution)/shard_map/pallas_call | solution.py:261
  87.1 7.4 %all-to-all-start = ((bf16[32,192,128]{2,1,0:T(8,128)(2,1)}), bf16[32,192,128]{2,1,0:T(8,128)(2,1)S(1)}, u32[]{:S(2)}, u32[]{:S(2)}) async-start(bf16[32,192,128]{2,1,0:T(8,128)(2,1)} %shard_map.98.refs_2_), calls=%async_computation | async-start | bytes 3145728 | tf_op jit(solution)/shard_map/all_to_all | solution.py:399
  95.9 2.2 %factors.1 = (bf16[256,256]{1,0:T(8,128)(2,1)}, bf16[256,256]{1,0:T(8,128)(2,1)}) custom-call(s32[8]{0:T(128)} %add_multiply_fusion.1.rows_ref, bf16[640,128]{1,0:T(8,128)(2,1)} %pack.1.refs_3_.refs_0_, bf16[640,128]{1,0:T(8,128)(2,1)} %copy-done.5, bf16[640,128]{1,0:T(8,128)(2,1)} %copy-done.9, bf16[640,128]{1,0:T(8,128)(2,1)} %copy-done.8, ...), custom_call_target="tpu_custom_call" | custom-call | tf_op jit(solution)/shard_map/factors/pallas_call | solution.py:189
  98.2 2.9 %shard_map.102 = bf16[32,128,128]{2,1,0:T(8,128)(2,1)} custom-call(bf16[32,128,128]{2,1,0:T(8,128)(2,1)} %copy-done.3, bf16[256,256]{1,0:T(8,128)(2,1)} %get-tuple-element.33.factor_ref, f32[256,8]{1,0:T(8,128)} %copy.15.twiddle_ref), custom_call_target="tpu_custom_call" | custom-call | tf_op jit(solution)/shard_map/pallas_call | solution.py:222
  101.1 16.1 %all-to-all-done.parts_ref.recv_ref = bf16[32,192,128]{2,1,0:T(8,128)(2,1)S(1)} async-done(((bf16[32,192,128]{2,1,0:T(8,128)(2,1)}), bf16[32,192,128]{2,1,0:T(8,128)(2,1)S(1)}, u32[]{:S(2)}, u32[]{:S(2)}) %all-to-all-start) | async-done | bytes 1572896 | tf_op jit(solution)/shard_map/all_to_all | solution.py:399
  117.2 5.5 %all-to-all-start.3 = ((bf16[32,128,128]{2,1,0:T(8,128)(2,1)}), bf16[32,128,128]{2,1,0:T(8,128)(2,1)S(1)}, u32[]{:S(2)}, u32[]{:S(2)}) async-start(bf16[32,128,128]{2,1,0:T(8,128)(2,1)} %shard_map.102), calls=%async_computation.3 | async-start | bytes 2097152 | tf_op jit(solution)/shard_map/all_to_all | solution.py:399
  124.5 4.1 %collective-permute-start.11 = (f32[16,128]{1,0:T(8,128)}, f32[16,128]{1,0:T(8,128)S(1)}, u32[]{:S(2)}, u32[]{:S(2)}) collective-permute-start(f32[16,128]{1,0:T(8,128)} %get-tuple-element.31), channel_id=1, source_target_pairs={{64,0},{96,32},{128,64},{160,96},{192,128},{224,160},{0,192},{32,2... | collective-permute-start | bytes 24584 | tf_op jit(solution)/shard_map/ppermute | solution.py:396
  129.7 2.9 %shard_map.100.refs_4_ = bf16[32,144,128]{2,1,0:T(8,128)(2,1)} custom-call(bf16[32,192,128]{2,1,0:T(8,128)(2,1)} %copy-done, bf16[256,256]{1,0:T(8,128)(2,1)} %get-tuple-element.33.factor_ref, f32[256,8]{1,0:T(8,128)} %copy.15.twiddle_ref), custom_call_target="tpu_custom_call" | custom-call | tf_op jit(solution)/shard_map/pallas_call | solution.py:222
  133.7 2.7 %collective-permute-done.12.refs_3_ = f32[16,128]{1,0:T(8,128)S(1)} collective-permute-done((f32[16,128]{1,0:T(8,128)}, f32[16,128]{1,0:T(8,128)S(1)}, u32[]{:S(2)}, u32[]{:S(2)}) %collective-permute-start.12) | collective-permute-done | bytes 8224 | tf_op jit(solution)/shard_map/ppermute | solution.py:396
  138.4 8.3 %all-to-all-start.1 = ((bf16[32,144,128]{2,1,0:T(8,128)(2,1)}), bf16[32,144,128]{2,1,0:T(8,128)(2,1)S(1)}, u32[]{:S(2)}, u32[]{:S(2)}) async-start(bf16[32,144,128]{2,1,0:T(8,128)(2,1)} %shard_map.101), calls=%async_computation.1 | async-start | bytes 2359296 | tf_op jit(solution)/shard_map/all_to_all | solution.py:399
  147.3 3.6 %shard_map.103.refs_5_ = bf16[2048,512]{1,0:T(8,128)(2,1)} custom-call(s32[2]{0:T(128)} %pad_add_fusion.1.refs_0_, bf16[32,128,128]{2,1,0:T(8,128)(2,1)} %copy-done.2, bf16[32,128,128]{2,1,0:T(8,128)(2,1)} %get-tuple-element.35.refs_2_, bf16[256,256]{1,0:T(8,128)(2,1)} %get-tuple-element.34.refs_3_), custom_call_target="tpu_custom_call" | custom-call | tf_op jit(solution)/shard_map/pallas_call | solution.py:361
  150.8 9.9 %all-to-all-done.1.refs_1_.refs_4_ = bf16[32,144,128]{2,1,0:T(8,128)(2,1)S(1)} async-done(((bf16[32,144,128]{2,1,0:T(8,128)(2,1)}), bf16[32,144,128]{2,1,0:T(8,128)(2,1)S(1)}, u32[]{:S(2)}, u32[]{:S(2)}) %all-to-all-start.1) | async-done | bytes 1179680 | tf_op jit(solution)/shard_map/all_to_all | solution.py:399
  161.8 3.7 %shard_map.104 = (bf16[2048,512]{1,0:T(8,128)(2,1)}, f32[256,128]{1,0:T(8,128)}, f32[256,128]{1,0:T(8,128)}) custom-call(s32[2]{0:T(128)} %pad_add_fusion.refs_0_, bf16[32,144,128]{2,1,0:T(8,128)(2,1)} %copy-done.1, bf16[32,192,128]{2,1,0:T(8,128)(2,1)} %shard_map.98.refs_2_, ...), custom_call_target="tpu_custom_call", output_to_operand_aliasing={{0}: (5, {})} | custom-call | tf_op jit(solution)/shard_map/pallas_call | solution.py:361
  (71 shorter events, 19.2 us)
Async XLA Ops:
  2.2 13.6 %collective-permute-start.5 = (bf16[640,128]{1,0:T(8,128)(2,1)}, bf16[640,128]{1,0:T(8,128)(2,1)S(1)}, u32[]{:S(2)}, u32[]{:S(2)}) collective-permute-start(bf16[640,128]{1,0:T(8,128)(2,1)} %pack.1.refs_3_.refs_0_), channel_id=1, source_target_pairs={{64,0},{96,32},{128,64},{160,96},{192,128},{224,160},{0,192},{32,2... | collective-permute-start | bytes 491528 | tf_op jit(solution)/shard_map/ppermute | solution.py:396
  8.5 7.3 %collective-permute-start.4 = (bf16[640,128]{1,0:T(8,128)(2,1)}, bf16[640,128]{1,0:T(8,128)(2,1)S(1)}, u32[]{:S(2)}, u32[]{:S(2)}) collective-permute-start(bf16[640,128]{1,0:T(8,128)(2,1)} %pack.1.refs_3_.refs_0_), channel_id=1, source_target_pairs={{0,32},{32,0},{64,96},{96,64},{128,160},{160,128},{192,224},{224,1... | collective-permute-start | bytes 491528 | tf_op jit(solution)/shard_map/ppermute | solution.py:392
  15.8 6.3 %copy-start.5 = (bf16[640,128]{1,0:T(8,128)(2,1)}, bf16[640,128]{1,0:T(8,128)(2,1)S(1)}, u32[]{:S(2)}) copy-start(bf16[640,128]{1,0:T(8,128)(2,1)S(1)} %collective-permute-done.5.refs_3_.refs_1_) | copy-start | bytes 491524
  15.8 6.3 %collective-permute-start.6 = (bf16[640,128]{1,0:T(8,128)(2,1)S(1)}, bf16[640,128]{1,0:T(8,128)(2,1)S(1)}, u32[]{:S(2)}, u32[]{:S(2)}) collective-permute-start(bf16[640,128]{1,0:T(8,128)(2,1)S(1)} %collective-permute-done.5.refs_3_.refs_1_), channel_id=1, source_target_pairs={{0,32},{32,0},{64,96},{96,64},{128,160},{160,128},{192,224},{224,1... | collective-permute-start | bytes 491528 | tf_op jit(solution)/shard_map/ppermute | solution.py:392
  28.4 7.7 %copy-start.4 = (bf16[640,128]{1,0:T(8,128)(2,1)S(1)}, bf16[640,128]{1,0:T(8,128)(2,1)}, u32[]{:S(2)}) copy-start(bf16[640,128]{1,0:T(8,128)(2,1)} %pack.1.refs_3_.refs_0_) | copy-start | bytes 491524
  28.4 14.6 %copy-start.19 = (f32[1,2,256,128]{3,2,1,0:T(8,128)S(1)}, f32[1,2,256,128]{3,2,1,0:T(8,128)}, u32[]{:S(2)}) copy-start(f32[1,2,256,128]{3,2,1,0:T(8,128)} %get-tuple-element.24) | copy-start | bytes 786436
  28.4 14.6 %copy-start.20 = (f32[1,2,256,128]{3,2,1,0:T(8,128)S(1)}, f32[1,2,256,128]{3,2,1,0:T(8,128)}, u32[]{:S(2)}) copy-start(f32[1,2,256,128]{3,2,1,0:T(8,128)} %get-tuple-element.25) | copy-start | bytes 786436
  28.4 57.7 %all-to-all-start.2 = ((bf16[32,128,128]{2,1,0:T(8,128)(2,1)}), bf16[32,128,128]{2,1,0:T(8,128)(2,1)S(1)}, u32[]{:S(2)}, u32[]{:S(2)}) async-start(bf16[32,128,128]{2,1,0:T(8,128)(2,1)} %get-tuple-element.35.refs_2_), calls=%async_computation.2 | async-start | bytes 2097152 | tf_op jit(solution)/shard_map/all_to_all | solution.py:399
  36.0 25.2 %collective-permute-start.2 = (bf16[640,128]{1,0:T(8,128)(2,1)S(1)}, bf16[640,128]{1,0:T(8,128)(2,1)S(1)}, u32[]{:S(2)}, u32[]{:S(2)}) collective-permute-start(bf16[640,128]{1,0:T(8,128)(2,1)S(1)} %copy-done.4), channel_id=1, source_target_pairs={{128,0},{160,32},{192,64},{224,96},{0,128},{32,160},{64,192},{96,2... | collective-permute-start | bytes 491528 | tf_op jit(solution)/shard_map/ppermute | solution.py:396
  40.3 26.4 %collective-permute-start = (bf16[640,128]{1,0:T(8,128)(2,1)S(1)}, bf16[640,128]{1,0:T(8,128)(2,1)S(1)}, u32[]{:S(2)}, u32[]{:S(2)}) collective-permute-start(bf16[640,128]{1,0:T(8,128)(2,1)S(1)} %copy-done.4), channel_id=1, source_target_pairs={{192,0},{224,32},{0,64},{32,96},{64,128},{96,160},{128,192},{160,2... | collective-permute-start | bytes 491528 | tf_op jit(solution)/shard_map/ppermute | solution.py:396
  43.0 24.3 %collective-permute-start.7 = (f32[1,2,256,128]{3,2,1,0:T(8,128)S(1)}, f32[1,2,256,128]{3,2,1,0:T(8,128)S(1)}, u32[]{:S(2)}, u32[]{:S(2)}) collective-permute-start(f32[1,2,256,128]{3,2,1,0:T(8,128)S(1)} %copy-done.19), channel_id=1, source_target_pairs={{0,32},{32,0},{64,96},{96,64},{128,160},{160,128},{192,224},{224,1... | collective-permute-start | bytes 786440 | tf_op jit(solution)/shard_map/ppermute | solution.py:392
  43.0 24.3 %collective-permute-start.8 = (f32[1,2,256,128]{3,2,1,0:T(8,128)S(1)}, f32[1,2,256,128]{3,2,1,0:T(8,128)S(1)}, u32[]{:S(2)}, u32[]{:S(2)}) collective-permute-start(f32[1,2,256,128]{3,2,1,0:T(8,128)S(1)} %copy-done.20), channel_id=1, source_target_pairs={{0,32},{32,0},{64,96},{96,64},{128,160},{160,128},{192,224},{224,1... | collective-permute-start | bytes 786440 | tf_op jit(solution)/shard_map/ppermute | solution.py:392
  61.3 8.7 %copy-start.8 = (bf16[640,128]{1,0:T(8,128)(2,1)}, bf16[640,128]{1,0:T(8,128)(2,1)S(1)}, u32[]{:S(2)}) copy-start(bf16[640,128]{1,0:T(8,128)(2,1)S(1)} %collective-permute-done.2.refs_5_.refs_3_) | copy-start | bytes 491524
  61.3 8.7 %collective-permute-start.3 = (bf16[640,128]{1,0:T(8,128)(2,1)S(1)}, bf16[640,128]{1,0:T(8,128)(2,1)S(1)}, u32[]{:S(2)}, u32[]{:S(2)}) collective-permute-start(bf16[640,128]{1,0:T(8,128)(2,1)S(1)} %collective-permute-done.2.refs_5_.refs_3_), channel_id=1, source_target_pairs={{0,32},{32,0},{64,96},{96,64},{128,160},{160,128},{192,224},{224,1... | collective-permute-start | bytes 491528 | tf_op jit(solution)/shard_map/ppermute | solution.py:392
  66.6 3.4 %collective-permute-start.1 = (bf16[640,128]{1,0:T(8,128)(2,1)S(1)}, bf16[640,128]{1,0:T(8,128)(2,1)S(1)}, u32[]{:S(2)}, u32[]{:S(2)}) collective-permute-start(bf16[640,128]{1,0:T(8,128)(2,1)S(1)} %collective-permute-done.refs_3_.refs_2_), channel_id=1, source_target_pairs={{0,32},{32,0},{64,96},{96,64},{128,160},{160,128},{192,224},{224,1... | collective-permute-start | bytes 491528 | tf_op jit(solution)/shard_map/ppermute | solution.py:392
  81.0 2.2 %collective-permute-start.9 = (f32[2,2,256,128]{3,2,1,0:T(8,128)}, f32[2,2,256,128]{3,2,1,0:T(8,128)S(1)}, u32[]{:S(2)}, u32[]{:S(2)}) collective-permute-start(f32[2,2,256,128]{3,2,1,0:T(8,128)} %get-tuple-element.27), channel_id=1, source_target_pairs={{0,32},{32,0},{64,96},{96,64},{128,160},{160,128},{192,224},{224,1... | collective-permute-start | bytes 1572872 | tf_op jit(solution)/shard_map/ppermute | solution.py:392
  86.1 8.4 %copy-start.18 = (f32[256,8]{0,1:T(8,128)S(1)}, f32[256,8]{0,1:T(8,128)}, u32[]{:S(2)}) copy-start(f32[256,8]{0,1:T(8,128)} %param.13) | copy-start | bytes 24580
  87.1 30.2 %all-to-all-start = ((bf16[32,192,128]{2,1,0:T(8,128)(2,1)}), bf16[32,192,128]{2,1,0:T(8,128)(2,1)S(1)}, u32[]{:S(2)}, u32[]{:S(2)}) async-start(bf16[32,192,128]{2,1,0:T(8,128)(2,1)} %shard_map.98.refs_2_), calls=%async_computation | async-start | bytes 3145728 | tf_op jit(solution)/shard_map/all_to_all | solution.py:399
  117.2 21.1 %all-to-all-start.3 = ((bf16[32,128,128]{2,1,0:T(8,128)(2,1)}), bf16[32,128,128]{2,1,0:T(8,128)(2,1)S(1)}, u32[]{:S(2)}, u32[]{:S(2)}) async-start(bf16[32,128,128]{2,1,0:T(8,128)(2,1)} %shard_map.102), calls=%async_computation.3 | async-start | bytes 2097152 | tf_op jit(solution)/shard_map/all_to_all | solution.py:399
  124.4 9.2 %collective-permute-start.10 = (f32[16,128]{1,0:T(8,128)}, f32[16,128]{1,0:T(8,128)S(1)}, u32[]{:S(2)}, u32[]{:S(2)}) collective-permute-start(f32[16,128]{1,0:T(8,128)} %get-tuple-element.30), channel_id=1, source_target_pairs={{192,0},{224,32},{0,64},{32,96},{64,128},{96,160},{128,192},{160,2... | collective-permute-start | bytes 24584 | tf_op jit(solution)/shard_map/ppermute | solution.py:396
  124.5 9.2 %collective-permute-start.11 = (f32[16,128]{1,0:T(8,128)}, f32[16,128]{1,0:T(8,128)S(1)}, u32[]{:S(2)}, u32[]{:S(2)}) collective-permute-start(f32[16,128]{1,0:T(8,128)} %get-tuple-element.31), channel_id=1, source_target_pairs={{64,0},{96,32},{128,64},{160,96},{192,128},{224,160},{0,192},{32,2... | collective-permute-start | bytes 24584 | tf_op jit(solution)/shard_map/ppermute | solution.py:396
  128.6 7.8 %collective-permute-start.12 = (f32[16,128]{1,0:T(8,128)}, f32[16,128]{1,0:T(8,128)S(1)}, u32[]{:S(2)}, u32[]{:S(2)}) collective-permute-start(f32[16,128]{1,0:T(8,128)} %get-tuple-element.32), channel_id=1, source_target_pairs={{128,0},{160,32},{192,64},{224,96},{0,128},{32,160},{64,192},{96,2... | collective-permute-start | bytes 24584 | tf_op jit(solution)/shard_map/ppermute | solution.py:396
  138.4 8.9 %copy-start.2 = (bf16[32,128,128]{2,1,0:T(8,128)(2,1)}, bf16[32,128,128]{2,1,0:T(8,128)(2,1)S(1)}, u32[]{:S(2)}) copy-start(bf16[32,128,128]{2,1,0:T(8,128)(2,1)S(1)} %all-to-all-done.3.refs_1_) | copy-start | bytes 3145732
  138.4 22.3 %all-to-all-start.1 = ((bf16[32,144,128]{2,1,0:T(8,128)(2,1)}), bf16[32,144,128]{2,1,0:T(8,128)(2,1)S(1)}, u32[]{:S(2)}, u32[]{:S(2)}) async-start(bf16[32,144,128]{2,1,0:T(8,128)(2,1)} %shard_map.101), calls=%async_computation.1 | async-start | bytes 2359296 | tf_op jit(solution)/shard_map/all_to_all | solution.py:399
  (14 other events, 21.9 us)

commit v2 on v1

--- a/solution.py
+++ b/solution.py
@@ -11,6 +11,13 @@
 NB = 4
 BF = jnp.bfloat16
 F32 = jnp.float32
+WHOLE = pl.BlockSpec(memory_space=pltpu.VMEM)
+
+
+def near_core(array):
+    return pltpu.with_memory_space_constraint(array, pltpu.VMEM)
+
+
 CUBIC = 0.044715
 
 
@@ -134,7 +141,6 @@
         jax.ShapeDtypeStruct((steps, 2, half_hidden, width), F32),
         jax.ShapeDtypeStruct((steps, 2, half_hidden, width), F32),
     )
-    piece = pl.BlockSpec(pieces[0].shape, lambda n, b: (0, 0))
     token_spec = pl.BlockSpec((tokens, width), lambda n, b: (0, b[n]))
     grad_spec = pl.BlockSpec((1, 2, half_hidden, width), lambda n, b: (n, 0, 0, 0))
     extra = [] if carried is None else [carried]
@@ -150,7 +156,7 @@
             num_scalar_prefetch=1,
             grid=(steps,),
             in_specs=[token_spec, token_spec]
-            + [piece] * (2 * steps)
+            + [WHOLE] * (2 * steps)
             + [pl.BlockSpec(memory_space=pl.ANY)] * len(extra),
             out_specs=(
                 pl.BlockSpec((groups, per_block, width), lambda n, b: (0, n + base, 0)),
@@ -163,7 +169,7 @@
             ],
         ),
         input_output_aliases={3 + 2 * steps: 0} if extra else {},
-    )(block_ids, saved, up, *pieces, *extra)
+    )(block_ids, saved, up, *[near_core(x) for x in pieces], *extra)
 
 
 def factor_kernel(rows_ref, *refs):
@@ -198,10 +204,12 @@
 
 def outer_kernel(recv_ref, factor_ref, twiddle_ref, *refs):
     out_ref, rows_ref = refs[-2:]
-    groups, per_block, width = recv_ref.shape
+    groups, per_block, width = out_ref.shape
     inner = twiddle_ref.shape[1]
     size = factor_ref.shape[0]
-    rows_ref[...] = recv_ref[...].reshape(groups * per_block, width).astype(F32)
+    start = pl.multiple_of(pl.program_id(0) * per_block, per_block)
+    recv = recv_ref[:, pl.ds(start, per_block), :]
+    rows_ref[...] = recv.reshape(groups * per_block, width).astype(F32)
     for j in range(0, inner, 2):
         pair = jnp.concatenate(
             [rows_ref[pl.ds(j + n, size, inner), :] for n in range(2)], axis=1
@@ -224,7 +232,7 @@
         out_shape=jax.ShapeDtypeStruct((groups, total_rows, width), BF),
         grid=(steps,),
         in_specs=[
-            pl.BlockSpec((groups, per_block, width), lambda b: (0, b, 0)),
+            WHOLE,
             pl.BlockSpec(factor_t.shape, lambda b: (0, 0)),
             pl.BlockSpec(twiddle.shape, lambda b: (0, 0)),
         ],
@@ -252,7 +260,7 @@
 def put_pair_sums(keeps, gots, groups, total_rows, start, carried):
     half_hidden, width = keeps[0].shape[2:]
     rows = sum(keep.shape[0] for keep in keeps) * 2 * (half_hidden // groups)
-    arrays = [*keeps, *gots]
+    arrays = [*keeps, *[near_core(x) for x in gots]]
     extra = [] if carried is None else [carried]
 
     def body(*refs):
@@ -262,7 +270,8 @@
         body,
         out_shape=jax.ShapeDtypeStruct((groups, total_rows, width), BF),
         grid=(1,),
-        in_specs=[pl.BlockSpec(x.shape, lambda n: (0, 0, 0, 0)) for x in arrays]
+        in_specs=[pl.BlockSpec(x.shape, lambda n: (0, 0, 0, 0)) for x in keeps]
+        + [WHOLE] * len(gots)
         + [pl.BlockSpec(memory_space=pl.ANY)] * len(extra),
         out_specs=pl.BlockSpec((groups, rows, width), lambda n: (0, start // rows, 0)),
         input_output_aliases={len(arrays): 0} if extra else {},
@@ -270,22 +279,23 @@
 
 
 def seq_sum_kernel(parts_ref, *out_refs):
-    total = jnp.sum(parts_ref[...].astype(F32), axis=0)
     rows = out_refs[0].shape[0]
+    start = parts_ref.shape[1] - rows * len(out_refs)
+    total = jnp.sum(parts_ref[:, start:, :].astype(F32), axis=0)
     for n, ref in enumerate(out_refs):
         ref[...] = total[n * rows : (n + 1) * rows]
 
 
 def seq_sums(recv, rows, count):
-    groups, all_rows, width = recv.shape
+    width = recv.shape[2]
     part = (rows // count, width)
     return pl.pallas_call(
         seq_sum_kernel,
         out_shape=[jax.ShapeDtypeStruct(part, F32)] * count,
         grid=(1,),
-        in_specs=[pl.BlockSpec((groups, rows, width), lambda n: (0, all_rows // rows - 1, 0))],
+        in_specs=[WHOLE],
         out_specs=[pl.BlockSpec(part, lambda n: (0, 0))] * count,
-    )(recv)
+    )(near_core(recv))
 
 
 def spread_kernel(scale, *refs):
@@ -303,21 +313,24 @@
         lambda *refs: spread_kernel(scale, *refs),
         out_shape=jax.ShapeDtypeStruct(buffer.shape, BF),
         grid=(1,),
-        in_specs=[pl.BlockSpec(x.shape, lambda n: (0, 0)) for x in parts]
+        in_specs=[WHOLE] * len(parts)
         + [pl.BlockSpec(memory_space=pl.ANY)],
         out_specs=pl.BlockSpec((groups, rows, width), lambda n: (0, all_rows // rows - 1, 0)),
         input_output_aliases={len(parts): 0},
-    )(*parts, buffer)
-
-
-def inner_kernel(has_rows, ids_ref, recv_ref, mixed_ref, factor_ref, *refs):
+    )(*[near_core(x) for x in parts], buffer)
+
+
+def inner_kernel(grad_rows, ids_ref, recv_ref, mixed_ref, factor_ref, *refs):
+    has_rows = grad_rows > 0
     rows_ref = refs[-1]
     out_ref = refs[-4] if has_rows else refs[-2]
-    groups, per_block, width = recv_ref.shape
+    groups, per_block, width = mixed_ref.shape
     size = factor_ref.shape[0]
     inner = size // groups
     outer = per_block // inner
-    rows_ref[...] = recv_ref[...].reshape(groups * per_block, width).astype(F32)
+    start = pl.multiple_of(pl.program_id(0) * per_block, per_block)
+    recv = recv_ref[:, pl.ds(start, per_block), :]
+    rows_ref[...] = recv.reshape(groups * per_block, width).astype(F32)
     for i in range(0, outer, 2):
         pair = jnp.concatenate(
             [rows_ref[pl.ds(i + n, size, outer), :] for n in range(2)], axis=1
@@ -331,45 +344,40 @@
                 own + back[:, n * width : (n + 1) * width]
             ).astype(BF)
     if has_rows:
-        grads = refs[0][...].astype(F32)
-        rows = grads.shape[1] // 2
+        grads = recv_ref[:, recv_ref.shape[1] - grad_rows :, :].astype(F32)
+        rows = grad_rows // 2
         for which in range(2):
             part = grads[:, which * rows : (which + 1) * rows]
             refs[-3 + which][...] = part.reshape(groups * rows, width)
 
 
 def inner_mix(block_ids, recv, mixed, factor_t, carried, per_block, grad_rows):
-    groups, all_rows, width = recv.shape
+    groups, _, width = recv.shape
     steps = block_ids.shape[0]
     spec = pl.BlockSpec((groups, per_block, width), lambda n, b: (0, n, 0))
     tokens = groups * per_block
     has_rows = carried is not None
-    extra = [recv, carried] if has_rows else []
+    extra = [carried] if has_rows else []
     out_shape = [jax.ShapeDtypeStruct((tokens, NB * width), BF)]
     out_specs = [pl.BlockSpec((tokens, width), lambda n, b: (0, b[n]))]
     extra_specs = []
     if has_rows:
-        extra_specs = [
-            pl.BlockSpec(
-                (groups, grad_rows, width), lambda n, b: (0, all_rows // grad_rows - 1, 0)
-            ),
-            pl.BlockSpec(memory_space=pl.ANY),
-        ]
+        extra_specs = [pl.BlockSpec(memory_space=pl.ANY)]
         full = (groups * grad_rows // 2, width)
         out_shape += [jax.ShapeDtypeStruct(full, F32)] * 2
         out_specs += [pl.BlockSpec(full, lambda n, b: (0, 0))] * 2
     return pl.pallas_call(
-        lambda *refs: inner_kernel(has_rows, *refs),
+        lambda *refs: inner_kernel(grad_rows if has_rows else 0, *refs),
         out_shape=out_shape,
         grid_spec=pltpu.PrefetchScalarGridSpec(
             num_scalar_prefetch=1,
             grid=(steps,),
-            in_specs=[spec, spec, pl.BlockSpec(factor_t.shape, lambda n, b: (0, 0))] + extra_specs,
+            in_specs=[WHOLE, spec, pl.BlockSpec(factor_t.shape, lambda n, b: (0, 0))] + extra_specs,
             out_specs=out_specs,
             scratch_shapes=[pltpu.VMEM((tokens, width), F32)],
         ),
-        input_output_aliases={5: 0} if has_rows else {},
-    )(block_ids, recv, mixed, factor_t, *extra)
+        input_output_aliases={4: 0} if has_rows else {},
+    )(block_ids, near_core(recv), mixed, factor_t, *extra)
 
 
 def shards(saved_mixed, out_grad, weight_in, weight_out, outer_factor, inner_factor, twiddle):
@@ -415,7 +423,7 @@
     chunks = [None, None]
     keeps = []
     gots = []
-    for n, (begin, end, target, base) in enumerate(calls):
+    for begin, end, target, base in calls:
         pieces = [side[step] for step in range(begin, end) for side in (near, far)]
         chunks[target], keep, send = block_steps(
             ids[begin:end],
@@ -430,12 +438,11 @@
         )
         keeps.append(keep)
         gots.append(swap(send))
-        if n > 0:
-            group = slice(0, 2) if n == 1 else slice(2, 3)
-            start = half_rows + (n - 1) * 2 * grad_rows
-            chunks[1] = put_pair_sums(
-                keeps[group], gots[group], seq_devices, rows_of[1], start, chunks[1]
-            )
+    for n, group in enumerate((slice(0, 2), slice(2, 3))):
+        start = half_rows + n * 2 * grad_rows
+        chunks[1] = put_pair_sums(
+            keeps[group], gots[group], seq_devices, rows_of[1], start, chunks[1]
+        )
 
     factor_rows = outer_factor.shape[0]
     starts = jnp.concatenate([2 * ids + core, 2 * ids + 1 - core]).astype(jnp.int32) * factor_rows
@@ -444,7 +451,14 @@
     for half in range(2):
         arrived = exchange(chunks[half])
         buffers.append(
-            outer_mix(arrived, outer_t, twiddle, per_block, NB // 2, half_rows + half * grad_rows)
+            outer_mix(
+                arrived if half == 0 else near_core(arrived),
+                outer_t,
+                twiddle,
+                per_block,
+                NB // 2,
+                half_rows + half * grad_rows,
+            )
         )
     sums = seq_sums(arrived, NB * grad_rows, NB)
     parts = [sums[0]]

time: 166 us -> 163 us (0.982)
  local copies, waits for them, and re-layouts: 7.68 us -> 2.83 us
  starting transfers between devices: 48.3 us -> 52.4 us
  Pallas kernels: 44.8 us -> 42 us
    unnamed x43 -> x29, local copies, waits for them, and re-layouts: 7.68 us -> 2.83 us
    ppermute x6, starting transfers between devices: 18.5 us -> 21.6 us  [from_chip(): return lax.ppermute(piece, 'dp', pairs)]
    ppermute x6, waiting for transfers between devices: 34.1 us -> 31.5 us  [from_chip(): return lax.ppermute(piece, 'dp', pairs)]
    all_to_all x4, waiting for transfers between devices: 26 us -> 27.7 us  [exchange(): return lax.all_to_all(array, 'seq', split_axis=0, concat_axis=0, tiled=True)]
  transfers between devices with their start and end apart: 17 -> 17, of which waited for: 8 -> 10; matrix products, arithmetic and copies ran while one was open for 2% -> 2% of each run, Pallas kernels for 21% -> 19%
where the time goes in v2:
time: 163 us; the launch traced here: 162 us
  waiting for transfers between devices  61.9 us (38%)
  starting transfers between devices  52.4 us (32%)
  Pallas kernels  42 us (26%)
  local copies, waits for them, and re-layouts  2.83 us (2%)
  other arithmetic  1.89 us (1%)
    ppermute x6, waiting for transfers between devices, from_chip(): return lax.ppermute(piece, 'dp', pairs)  31.5 us
    all_to_all x4, starting transfers between devices, exchange(): return lax.all_to_all(array, 'seq', split_axis=0, concat_axis=0, tiled=True)  29.5 us
    all_to_all x4, waiting for transfers between devices, exchange(): return lax.all_to_all(array, 'seq', split_axis=0, concat_axis=0, tiled=True)  27.7 us
    ppermute x6, starting transfers between devices, from_chip(): return lax.ppermute(piece, 'dp', pairs)  21.6 us
    pallas_call x3, Pallas kernels, block_steps(): pl.pallas_call(body, out_shape=out_shape, grid_spec=pltpu.PrefetchScalarG...  20.5 us
    pallas_call x2, Pallas kernels, inner_mix(): pl.pallas_call(lambda *refs: inner_kernel(grad_rows if has_rows else 0, *...  6.85 us
    pallas_call x2, Pallas kernels, outer_mix(): pl.pallas_call(outer_kernel, out_shape=jax.ShapeDtypeStruct((groups, tota...  5.91 us
    pallas_call x2, Pallas kernels, put_pair_sums(): pl.pallas_call(body, out_shape=jax.ShapeDtypeStruct((groups, total_rows,...  3.67 us
  transfers between devices with their start and end apart: 17, of which 10 were waited for; matrix products, arithmetic and copies ran while one was open for 2% of the time, Pallas kernels for 19%

profile of v2, /device:TPU:8, one launch (start us, length us, event | category | flops | bytes accessed | tf_op | source)
XLA Modules:
  0.0 161.9 jit_solution(305001476499709065)
XLA Ops:
  2.2 6.3 %collective-permute-start.6 = (bf16[640,128]{1,0:T(8,128)(2,1)}, bf16[640,128]{1,0:T(8,128)(2,1)S(1)}, u32[]{:S(2)}, u32[]{:S(2)}) collective-permute-start(bf16[640,128]{1,0:T(8,128)(2,1)} %pack.1.refs_3_.refs_0_), channel_id=1, source_target_pairs={{64,0},{96,32},{128,64},{160,96},{192,128},{224,160},{0,192},{32,2... | collective-permute-start | bytes 491528 | tf_op jit(solution)/shard_map/ppermute | solution.py:404
  8.5 7.3 %collective-permute-done.6.refs_3_.refs_1_ = bf16[640,128]{1,0:T(8,128)(2,1)S(1)} collective-permute-done((bf16[640,128]{1,0:T(8,128)(2,1)}, bf16[640,128]{1,0:T(8,128)(2,1)S(1)}, u32[]{:S(2)}, u32[]{:S(2)}) %collective-permute-start.6) | collective-permute-done | bytes 163872 | tf_op jit(solution)/shard_map/ppermute | solution.py:404
  16.8 5.5 %shard_map.95 = (bf16[32,128,128]{2,1,0:T(8,128)(2,1)}, f32[1,2,256,128]{3,2,1,0:T(8,128)}, f32[1,2,256,128]{3,2,1,0:T(8,128)}) custom-call(s32[1]{0:T(128)} %bitcast.4.refs_0_, bf16[2048,512]{1,0:T(8,128)(2,1)} %bitcast.7, bf16[2048,512]{1,0:T(8,128)(2,1)} %bitcast.10, bf16[640,128]{1,0:T(8,128)(2,1)S(1)} %copy-done, ...), custom_call_target="tpu_custom_call" | custom-call | tf_op jit(solution)/shard_map/pallas_call | solution.py:152
  22.3 5.6 %shard_map.96 = (bf16[32,128,128]{2,1,0:T(8,128)(2,1)}, f32[1,2,256,128]{3,2,1,0:T(8,128)}, f32[1,2,256,128]{3,2,1,0:T(8,128)}) custom-call(s32[1]{0:T(128)} %bitcast.5.refs_0_, bf16[2048,512]{1,0:T(8,128)(2,1)} %bitcast.8, bf16[2048,512]{1,0:T(8,128)(2,1)} %bitcast.11, ...), custom_call_target="tpu_custom_call", output_to_operand_aliasing={{0}: (5, {})} | custom-call | tf_op jit(solution)/shard_map/pallas_call | solution.py:152
  27.9 7.7 %all-to-all-start.2 = ((bf16[32,128,128]{2,1,0:T(8,128)(2,1)}), bf16[32,128,128]{2,1,0:T(8,128)(2,1)S(1)}, u32[]{:S(2)}, u32[]{:S(2)}) async-start(bf16[32,128,128]{2,1,0:T(8,128)(2,1)} %get-tuple-element.35.refs_2_), calls=%async_computation.2 | async-start | bytes 2097152 | tf_op jit(solution)/shard_map/all_to_all | solution.py:407
  35.6 2.1 %collective-permute-start = (bf16[640,128]{1,0:T(8,128)(2,1)S(1)}, bf16[640,128]{1,0:T(8,128)(2,1)S(1)}, u32[]{:S(2)}, u32[]{:S(2)}) collective-permute-start(bf16[640,128]{1,0:T(8,128)(2,1)S(1)} %copy-done.1), channel_id=1, source_target_pairs={{192,0},{224,32},{0,64},{32,96},{64,128},{96,160},{128,192},{160,2... | collective-permute-start | bytes 491528 | tf_op jit(solution)/shard_map/ppermute | solution.py:404
  37.7 4.8 %collective-permute-start.2 = (bf16[640,128]{1,0:T(8,128)(2,1)S(1)}, bf16[640,128]{1,0:T(8,128)(2,1)S(1)}, u32[]{:S(2)}, u32[]{:S(2)}) collective-permute-start(bf16[640,128]{1,0:T(8,128)(2,1)S(1)} %copy-done.1), channel_id=1, source_target_pairs={{128,0},{160,32},{192,64},{224,96},{0,128},{32,160},{64,192},{96,2... | collective-permute-start | bytes 491528 | tf_op jit(solution)/shard_map/ppermute | solution.py:404
  42.5 20.9 %collective-permute-done.refs_3_.refs_2_ = bf16[640,128]{1,0:T(8,128)(2,1)S(1)} collective-permute-done((bf16[640,128]{1,0:T(8,128)(2,1)S(1)}, bf16[640,128]{1,0:T(8,128)(2,1)S(1)}, u32[]{:S(2)}, u32[]{:S(2)}) %collective-permute-start) | collective-permute-done | bytes 163872 | tf_op jit(solution)/shard_map/ppermute | solution.py:404
  65.1 9.4 %shard_map.94 = (bf16[32,192,128]{2,1,0:T(8,128)(2,1)}, f32[2,2,256,128]{3,2,1,0:T(8,128)}, f32[2,2,256,128]{3,2,1,0:T(8,128)}) custom-call(s32[2]{0:T(128)} %pad_add_fusion.refs_0_, bf16[2048,512]{1,0:T(8,128)(2,1)} %bitcast.9, bf16[2048,512]{1,0:T(8,128)(2,1)} %bitcast.12, bf16[640,128]{1,0:T(8,128)(2,1)S(1)} %collective-permute-done.refs_3_.refs_2_, ...), custom_call_target="tpu_custom_call" | custom-call | tf_op jit(solution)/shard_map/pallas_call | solution.py:152
  77.6 1.8 %shard_map.97.refs_2_ = bf16[32,192,128]{2,1,0:T(8,128)(2,1)} custom-call(f32[1,2,256,128]{3,2,1,0:T(8,128)} %get-tuple-element.23.refs_0_, f32[1,2,256,128]{3,2,1,0:T(8,128)} %get-tuple-element.25.refs_1_, f32[1,2,256,128]{3,2,1,0:T(8,128)S(1)} %collective-permute-done.8.refs_2_, ...), custom_call_target="tpu_custom_call", output_to_operand_aliasing={{}: (4, {})} | custom-call | tf_op jit(solution)/shard_map/pallas_call | solution.py:269
  79.4 1.8 %shard_map.98.refs_2_ = bf16[32,192,128]{2,1,0:T(8,128)(2,1)} custom-call(f32[2,2,256,128]{3,2,1,0:T(8,128)} %get-tuple-element.21.refs_0_, f32[2,2,256,128]{3,2,1,0:T(8,128)S(1)} %collective-permute-done.4.refs_1_, bf16[32,192,128]{2,1,0:T(8,128)(2,1)} %shard_map.97.refs_2_), custom_call_target="tpu_custom_call", output_to_operand_aliasing={{}: (2, {})} | custom-call | tf_op jit(solution)/shard_map/pallas_call | solution.py:269
  82.2 7.4 %all-to-all-start = ((bf16[32,192,128]{2,1,0:T(8,128)(2,1)}), bf16[32,192,128]{2,1,0:T(8,128)(2,1)S(1)}, u32[]{:S(2)}, u32[]{:S(2)}) async-start(bf16[32,192,128]{2,1,0:T(8,128)(2,1)} %shard_map.98.refs_2_), calls=%async_computation | async-start | bytes 3145728 | tf_op jit(solution)/shard_map/all_to_all | solution.py:407
  91.1 2.2 %factors.1 = (bf16[256,256]{1,0:T(8,128)(2,1)}, bf16[256,256]{1,0:T(8,128)(2,1)}) custom-call(s32[8]{0:T(128)} %add_multiply_fusion.1.rows_ref, bf16[640,128]{1,0:T(8,128)(2,1)} %pack.1.refs_3_.refs_0_, bf16[640,128]{1,0:T(8,128)(2,1)} %copy-done.2, bf16[640,128]{1,0:T(8,128)(2,1)} %copy-done.5, bf16[640,128]{1,0:T(8,128)(2,1)} %copy-done.6, ...), custom_call_target="tpu_custom_call" | custom-call | tf_op jit(solution)/shard_map/factors/pallas_call | solution.py:195
  93.3 3.1 %shard_map.102 = bf16[32,128,128]{2,1,0:T(8,128)(2,1)} custom-call(bf16[32,128,128]{2,1,0:T(8,128)(2,1)} %copy-done.10, bf16[256,256]{1,0:T(8,128)(2,1)} %get-tuple-element.33.factor_ref, f32[256,8]{1,0:T(8,128)} %copy.15.twiddle_ref), custom_call_target="tpu_custom_call" | custom-call | tf_op jit(solution)/shard_map/pallas_call | solution.py:230
  96.5 15.8 %all-to-all-done.parts_ref.recv_ref = bf16[32,192,128]{2,1,0:T(8,128)(2,1)S(1)} async-done(((bf16[32,192,128]{2,1,0:T(8,128)(2,1)}), bf16[32,192,128]{2,1,0:T(8,128)(2,1)S(1)}, u32[]{:S(2)}, u32[]{:S(2)}) %all-to-all-start) | async-done | bytes 1572896 | tf_op jit(solution)/shard_map/all_to_all | solution.py:407
  112.3 5.6 %all-to-all-start.3 = ((bf16[32,128,128]{2,1,0:T(8,128)(2,1)}), bf16[32,128,128]{2,1,0:T(8,128)(2,1)S(1)}, u32[]{:S(2)}, u32[]{:S(2)}) async-start(bf16[32,128,128]{2,1,0:T(8,128)(2,1)} %shard_map.102), calls=%async_computation.3 | async-start | bytes 2097152 | tf_op jit(solution)/shard_map/all_to_all | solution.py:407
  118.5 4.7 %collective-permute-start.10 = (f32[16,128]{1,0:T(8,128)}, f32[16,128]{1,0:T(8,128)S(1)}, u32[]{:S(2)}, u32[]{:S(2)}) collective-permute-start(f32[16,128]{1,0:T(8,128)} %get-tuple-element.30), channel_id=1, source_target_pairs={{192,0},{224,32},{0,64},{32,96},{64,128},{96,160},{128,192},{160,2... | collective-permute-start | bytes 24584 | tf_op jit(solution)/shard_map/ppermute | solution.py:404
  123.3 3.6 %collective-permute-start.12 = (f32[16,128]{1,0:T(8,128)}, f32[16,128]{1,0:T(8,128)S(1)}, u32[]{:S(2)}, u32[]{:S(2)}) collective-permute-start(f32[16,128]{1,0:T(8,128)} %get-tuple-element.32), channel_id=1, source_target_pairs={{128,0},{160,32},{192,64},{224,96},{0,128},{32,160},{64,192},{96,2... | collective-permute-start | bytes 24584 | tf_op jit(solution)/shard_map/ppermute | solution.py:404
  126.9 2.8 %shard_map.100.refs_4_ = bf16[32,144,128]{2,1,0:T(8,128)(2,1)} custom-call(bf16[32,192,128]{2,1,0:T(8,128)(2,1)S(1)} %all-to-all-done.parts_ref.recv_ref, bf16[256,256]{1,0:T(8,128)(2,1)} %get-tuple-element.33.factor_ref, f32[256,8]{1,0:T(8,128)} %copy.15.twiddle_ref), custom_call_target="tpu_custom_call" | custom-call | tf_op jit(solution)/shard_map/pallas_call | solution.py:230
  129.7 3.2 %collective-permute-done.10.refs_1_ = f32[16,128]{1,0:T(8,128)S(1)} collective-permute-done((f32[16,128]{1,0:T(8,128)}, f32[16,128]{1,0:T(8,128)S(1)}, u32[]{:S(2)}, u32[]{:S(2)}) %collective-permute-start.10) | collective-permute-done | bytes 8224 | tf_op jit(solution)/shard_map/ppermute | solution.py:404
  134.1 8.9 %all-to-all-start.1 = ((bf16[32,144,128]{2,1,0:T(8,128)(2,1)}), bf16[32,144,128]{2,1,0:T(8,128)(2,1)S(1)}, u32[]{:S(2)}, u32[]{:S(2)}) async-start(bf16[32,144,128]{2,1,0:T(8,128)(2,1)} %shard_map.101), calls=%async_computation.1 | async-start | bytes 2359296 | tf_op jit(solution)/shard_map/all_to_all | solution.py:407
  143.6 3.4 %shard_map.103.refs_4_ = bf16[2048,512]{1,0:T(8,128)(2,1)} custom-call(s32[2]{0:T(128)} %pad_add_fusion.1.refs_0_, bf16[32,128,128]{2,1,0:T(8,128)(2,1)S(1)} %all-to-all-done.3.refs_1_, bf16[32,128,128]{2,1,0:T(8,128)(2,1)} %get-tuple-element.35.refs_2_, bf16[256,256]{1,0:T(8,128)(2,1)} %get-tuple-element.34.refs_3_), custom_call_target="tpu_custom_call" | custom-call | tf_op jit(solution)/shard_map/pallas_call | solution.py:369
  147.0 11.4 %all-to-all-done.1.refs_1_ = bf16[32,144,128]{2,1,0:T(8,128)(2,1)S(1)} async-done(((bf16[32,144,128]{2,1,0:T(8,128)(2,1)}), bf16[32,144,128]{2,1,0:T(8,128)(2,1)S(1)}, u32[]{:S(2)}, u32[]{:S(2)}) %all-to-all-start.1) | async-done | bytes 1179680 | tf_op jit(solution)/shard_map/all_to_all | solution.py:407
  158.4 3.5 %shard_map.104 = (bf16[2048,512]{1,0:T(8,128)(2,1)}, f32[256,128]{1,0:T(8,128)}, f32[256,128]{1,0:T(8,128)}) custom-call(s32[2]{0:T(128)} %pad_add_fusion.refs_0_, bf16[32,144,128]{2,1,0:T(8,128)(2,1)S(1)} %all-to-all-done.1.refs_1_, bf16[32,192,128]{2,1,0:T(8,128)(2,1)} %shard_map.98.refs_2_, ...), custom_call_target="tpu_custom_call", output_to_operand_aliasing={{0}: (4, {})} | custom-call | tf_op jit(solution)/shard_map/pallas_call | solution.py:369
  (57 shorter events, 12.3 us)
Async XLA Ops:
  2.2 13.6 %collective-permute-start.6 = (bf16[640,128]{1,0:T(8,128)(2,1)}, bf16[640,128]{1,0:T(8,128)(2,1)S(1)}, u32[]{:S(2)}, u32[]{:S(2)}) collective-permute-start(bf16[640,128]{1,0:T(8,128)(2,1)} %pack.1.refs_3_.refs_0_), channel_id=1, source_target_pairs={{64,0},{96,32},{128,64},{160,96},{192,128},{224,160},{0,192},{32,2... | collective-permute-start | bytes 491528 | tf_op jit(solution)/shard_map/ppermute | solution.py:404
  8.5 7.3 %collective-permute-start.5 = (bf16[640,128]{1,0:T(8,128)(2,1)}, bf16[640,128]{1,0:T(8,128)(2,1)S(1)}, u32[]{:S(2)}, u32[]{:S(2)}) collective-permute-start(bf16[640,128]{1,0:T(8,128)(2,1)} %pack.1.refs_3_.refs_0_), channel_id=1, source_target_pairs={{0,32},{32,0},{64,96},{96,64},{128,160},{160,128},{192,224},{224,1... | collective-permute-start | bytes 491528 | tf_op jit(solution)/shard_map/ppermute | solution.py:400
  15.8 6.5 %collective-permute-start.7 = (bf16[640,128]{1,0:T(8,128)(2,1)S(1)}, bf16[640,128]{1,0:T(8,128)(2,1)S(1)}, u32[]{:S(2)}, u32[]{:S(2)}) collective-permute-start(bf16[640,128]{1,0:T(8,128)(2,1)S(1)} %collective-permute-done.6.refs_3_.refs_1_), channel_id=1, source_target_pairs={{0,32},{32,0},{64,96},{96,64},{128,160},{160,128},{192,224},{224,1... | collective-permute-start | bytes 491528 | tf_op jit(solution)/shard_map/ppermute | solution.py:400
  27.9 53.3 %all-to-all-start.2 = ((bf16[32,128,128]{2,1,0:T(8,128)(2,1)}), bf16[32,128,128]{2,1,0:T(8,128)(2,1)S(1)}, u32[]{:S(2)}, u32[]{:S(2)}) async-start(bf16[32,128,128]{2,1,0:T(8,128)(2,1)} %get-tuple-element.35.refs_2_), calls=%async_computation.2 | async-start | bytes 2097152 | tf_op jit(solution)/shard_map/all_to_all | solution.py:407
  35.6 27.9 %collective-permute-start = (bf16[640,128]{1,0:T(8,128)(2,1)S(1)}, bf16[640,128]{1,0:T(8,128)(2,1)S(1)}, u32[]{:S(2)}, u32[]{:S(2)}) collective-permute-start(bf16[640,128]{1,0:T(8,128)(2,1)S(1)} %copy-done.1), channel_id=1, source_target_pairs={{192,0},{224,32},{0,64},{32,96},{64,128},{96,160},{128,192},{160,2... | collective-permute-start | bytes 491528 | tf_op jit(solution)/shard_map/ppermute | solution.py:404
  37.7 25.7 %collective-permute-start.2 = (bf16[640,128]{1,0:T(8,128)(2,1)S(1)}, bf16[640,128]{1,0:T(8,128)(2,1)S(1)}, u32[]{:S(2)}, u32[]{:S(2)}) collective-permute-start(bf16[640,128]{1,0:T(8,128)(2,1)S(1)} %copy-done.1), channel_id=1, source_target_pairs={{128,0},{160,32},{192,64},{224,96},{0,128},{32,160},{64,192},{96,2... | collective-permute-start | bytes 491528 | tf_op jit(solution)/shard_map/ppermute | solution.py:404
  63.4 11.1 %copy-start.5 = (bf16[640,128]{1,0:T(8,128)(2,1)}, bf16[640,128]{1,0:T(8,128)(2,1)S(1)}, u32[]{:S(2)}) copy-start(bf16[640,128]{1,0:T(8,128)(2,1)S(1)} %collective-permute-done.refs_3_.refs_2_) | copy-start | bytes 491524
  63.4 1.4 collective-permute-start.1
  63.4 11.1 %copy-start.6 = (bf16[640,128]{1,0:T(8,128)(2,1)}, bf16[640,128]{1,0:T(8,128)(2,1)S(1)}, u32[]{:S(2)}) copy-start(bf16[640,128]{1,0:T(8,128)(2,1)S(1)} %collective-permute-done.2.refs_5_.refs_3_) | copy-start | bytes 491524
  63.5 1.7 %collective-permute-start.3 = (bf16[640,128]{1,0:T(8,128)(2,1)S(1)}, bf16[640,128]{1,0:T(8,128)(2,1)S(1)}, u32[]{:S(2)}, u32[]{:S(2)}) collective-permute-start(bf16[640,128]{1,0:T(8,128)(2,1)S(1)} %collective-permute-done.2.refs_5_.refs_3_), channel_id=1, source_target_pairs={{0,32},{32,0},{64,96},{96,64},{128,160},{160,128},{192,224},{224,1... | collective-permute-start | bytes 491528 | tf_op jit(solution)/shard_map/ppermute | solution.py:400
  64.5 10.4 %copy-start.12 = (f32[1,2,256,128]{3,2,1,0:T(8,128)S(1)}, f32[1,2,256,128]{3,2,1,0:T(8,128)}, u32[]{:S(2)}) copy-start(f32[1,2,256,128]{3,2,1,0:T(8,128)} %get-tuple-element.26) | copy-start | bytes 786436
  64.5 10.7 %copy-start.13 = (f32[1,2,256,128]{3,2,1,0:T(8,128)S(1)}, f32[1,2,256,128]{3,2,1,0:T(8,128)}, u32[]{:S(2)}) copy-start(f32[1,2,256,128]{3,2,1,0:T(8,128)} %get-tuple-element.27) | copy-start | bytes 786436
  64.8 9.7 %copy-start.7 = (bf16[640,128]{1,0:T(8,128)(2,1)}, bf16[640,128]{1,0:T(8,128)(2,1)S(1)}, u32[]{:S(2)}) copy-start(bf16[640,128]{1,0:T(8,128)(2,1)S(1)} %collective-permute-done.1.refs_4_.refs_6_) | copy-start | bytes 491524
  65.1 9.5 %copy-start.8 = (bf16[640,128]{1,0:T(8,128)(2,1)}, bf16[640,128]{1,0:T(8,128)(2,1)S(1)}, u32[]{:S(2)}) copy-start(bf16[640,128]{1,0:T(8,128)(2,1)S(1)} %collective-permute-done.3.refs_6_.refs_7_) | copy-start | bytes 491524
  74.6 4.8 %collective-permute-start.4 = (f32[2,2,256,128]{3,2,1,0:T(8,128)}, f32[2,2,256,128]{3,2,1,0:T(8,128)S(1)}, u32[]{:S(2)}, u32[]{:S(2)}) collective-permute-start(f32[2,2,256,128]{3,2,1,0:T(8,128)} %get-tuple-element.22), channel_id=1, source_target_pairs={{0,32},{32,0},{64,96},{96,64},{128,160},{160,128},{192,224},{224,1... | collective-permute-start | bytes 1572872 | tf_op jit(solution)/shard_map/ppermute | solution.py:400
  74.9 2.3 %collective-permute-start.8 = (f32[1,2,256,128]{3,2,1,0:T(8,128)S(1)}, f32[1,2,256,128]{3,2,1,0:T(8,128)S(1)}, u32[]{:S(2)}, u32[]{:S(2)}) collective-permute-start(f32[1,2,256,128]{3,2,1,0:T(8,128)S(1)} %copy-done.12), channel_id=1, source_target_pairs={{0,32},{32,0},{64,96},{96,64},{128,160},{160,128},{192,224},{224,1... | collective-permute-start | bytes 786440 | tf_op jit(solution)/shard_map/ppermute | solution.py:400
  75.2 2.4 %collective-permute-start.9 = (f32[1,2,256,128]{3,2,1,0:T(8,128)S(1)}, f32[1,2,256,128]{3,2,1,0:T(8,128)S(1)}, u32[]{:S(2)}, u32[]{:S(2)}) collective-permute-start(f32[1,2,256,128]{3,2,1,0:T(8,128)S(1)} %copy-done.13), channel_id=1, source_target_pairs={{0,32},{32,0},{64,96},{96,64},{128,160},{160,128},{192,224},{224,1... | collective-permute-start | bytes 786440 | tf_op jit(solution)/shard_map/ppermute | solution.py:400
  82.2 30.0 %all-to-all-start = ((bf16[32,192,128]{2,1,0:T(8,128)(2,1)}), bf16[32,192,128]{2,1,0:T(8,128)(2,1)S(1)}, u32[]{:S(2)}, u32[]{:S(2)}) async-start(bf16[32,192,128]{2,1,0:T(8,128)(2,1)} %shard_map.98.refs_2_), calls=%async_computation | async-start | bytes 3145728 | tf_op jit(solution)/shard_map/all_to_all | solution.py:407
  112.3 21.9 %all-to-all-start.3 = ((bf16[32,128,128]{2,1,0:T(8,128)(2,1)}), bf16[32,128,128]{2,1,0:T(8,128)(2,1)S(1)}, u32[]{:S(2)}, u32[]{:S(2)}) async-start(bf16[32,128,128]{2,1,0:T(8,128)(2,1)} %shard_map.102), calls=%async_computation.3 | async-start | bytes 2097152 | tf_op jit(solution)/shard_map/all_to_all | solution.py:407
  118.5 14.4 %copy-start.9 = (f32[16,128]{1,0:T(8,128)S(1)}, f32[16,128]{1,0:T(8,128)}, u32[]{:S(2)}) copy-start(f32[16,128]{1,0:T(8,128)} %get-tuple-element.29.refs_0_) | copy-start | bytes 24580
  118.5 14.3 %collective-permute-start.10 = (f32[16,128]{1,0:T(8,128)}, f32[16,128]{1,0:T(8,128)S(1)}, u32[]{:S(2)}, u32[]{:S(2)}) collective-permute-start(f32[16,128]{1,0:T(8,128)} %get-tuple-element.30), channel_id=1, source_target_pairs={{192,0},{224,32},{0,64},{32,96},{64,128},{96,160},{128,192},{160,2... | collective-permute-start | bytes 24584 | tf_op jit(solution)/shard_map/ppermute | solution.py:404
  123.3 9.6 %collective-permute-start.11 = (f32[16,128]{1,0:T(8,128)}, f32[16,128]{1,0:T(8,128)S(1)}, u32[]{:S(2)}, u32[]{:S(2)}) collective-permute-start(f32[16,128]{1,0:T(8,128)} %get-tuple-element.31), channel_id=1, source_target_pairs={{64,0},{96,32},{128,64},{160,96},{192,128},{224,160},{0,192},{32,2... | collective-permute-start | bytes 24584 | tf_op jit(solution)/shard_map/ppermute | solution.py:404
  123.3 9.6 %collective-permute-start.12 = (f32[16,128]{1,0:T(8,128)}, f32[16,128]{1,0:T(8,128)S(1)}, u32[]{:S(2)}, u32[]{:S(2)}) collective-permute-start(f32[16,128]{1,0:T(8,128)} %get-tuple-element.32), channel_id=1, source_target_pairs={{128,0},{160,32},{192,64},{224,96},{0,128},{32,160},{64,192},{96,2... | collective-permute-start | bytes 24584 | tf_op jit(solution)/shard_map/ppermute | solution.py:404
  134.1 24.3 %all-to-all-start.1 = ((bf16[32,144,128]{2,1,0:T(8,128)(2,1)}), bf16[32,144,128]{2,1,0:T(8,128)(2,1)S(1)}, u32[]{:S(2)}, u32[]{:S(2)}) async-start(bf16[32,144,128]{2,1,0:T(8,128)(2,1)} %shard_map.101), calls=%async_computation.1 | async-start | bytes 2359296 | tf_op jit(solution)/shard_map/all_to_all | solution.py:407
  (7 other events, 36.7 us)

commit v3 on v2

--- a/solution.py
+++ b/solution.py
@@ -19,6 +19,10 @@
 
 
 CUBIC = 0.044715
+
+
+def block_at(chip_ref, step):
+    return (chip_ref[0] + (step ^ (step >> 1))) % NB
 
 
 def gelu_parts(pre_act):
@@ -130,7 +134,7 @@
         send_ref[0, which] = acc_ref[2 + which].T
 
 
-def block_steps(block_ids, saved, up, pieces, groups, inner_size, total_rows, base, carried):
+def block_steps(chip, begin, saved, up, pieces, groups, inner_size, total_rows, base, carried):
     steps = len(pieces) // 2
     tokens, features = saved.shape
     width = features // NB
@@ -141,7 +145,7 @@
         jax.ShapeDtypeStruct((steps, 2, half_hidden, width), F32),
         jax.ShapeDtypeStruct((steps, 2, half_hidden, width), F32),
     )
-    token_spec = pl.BlockSpec((tokens, width), lambda n, b: (0, b[n]))
+    token_spec = pl.BlockSpec((tokens, width), lambda n, c: (0, block_at(c, n + begin)))
     grad_spec = pl.BlockSpec((1, 2, half_hidden, width), lambda n, b: (n, 0, 0, 0))
     extra = [] if carried is None else [carried]
 
@@ -169,7 +173,7 @@
             ],
         ),
         input_output_aliases={3 + 2 * steps: 0} if extra else {},
-    )(block_ids, saved, up, *[near_core(x) for x in pieces], *extra)
+    )(chip, saved, up, *[near_core(x) if n else x for n, x in enumerate(pieces)], *extra)
 
 
 def factor_kernel(rows_ref, *refs):
@@ -202,12 +206,12 @@
     )(row_starts, *pieces)
 
 
-def outer_kernel(recv_ref, factor_ref, twiddle_ref, *refs):
+def outer_kernel(first, recv_ref, factor_ref, twiddle_ref, *refs):
     out_ref, rows_ref = refs[-2:]
     groups, per_block, width = out_ref.shape
     inner = twiddle_ref.shape[1]
     size = factor_ref.shape[0]
-    start = pl.multiple_of(pl.program_id(0) * per_block, per_block)
+    start = pl.multiple_of((pl.program_id(0) + first) * per_block, per_block)
     recv = recv_ref[:, pl.ds(start, per_block), :]
     rows_ref[...] = recv.reshape(groups * per_block, width).astype(F32)
     for j in range(0, inner, 2):
@@ -225,20 +229,23 @@
         out_ref[:, j * step : (j + 2) * step, :] = jnp.concatenate(parts, axis=1).astype(BF)
 
 
-def outer_mix(recv, factor_t, twiddle, per_block, steps, total_rows):
+def outer_mix(recv, factor_t, twiddle, per_block, first, steps, total_rows, base, carried):
     groups, _, width = recv.shape
-    return pl.pallas_call(
-        outer_kernel,
+    extra = [] if carried is None else [carried]
+    return pl.pallas_call(
+        lambda *refs: outer_kernel(first, *refs),
         out_shape=jax.ShapeDtypeStruct((groups, total_rows, width), BF),
         grid=(steps,),
         in_specs=[
             WHOLE,
             pl.BlockSpec(factor_t.shape, lambda b: (0, 0)),
             pl.BlockSpec(twiddle.shape, lambda b: (0, 0)),
-        ],
-        out_specs=pl.BlockSpec((groups, per_block, width), lambda b: (0, b, 0)),
+        ]
+        + [pl.BlockSpec(memory_space=pl.ANY)] * len(extra),
+        out_specs=pl.BlockSpec((groups, per_block, width), lambda b: (0, b + base, 0)),
         scratch_shapes=[pltpu.VMEM((groups * per_block, width), F32)],
-    )(recv, factor_t, twiddle)
+        input_output_aliases={3: 0} if extra else {},
+    )(recv, factor_t, twiddle, *extra)
 
 
 def pair_add_kernel(*refs):
@@ -260,6 +267,7 @@
 def put_pair_sums(keeps, gots, groups, total_rows, start, carried):
     half_hidden, width = keeps[0].shape[2:]
     rows = sum(keep.shape[0] for keep in keeps) * 2 * (half_hidden // groups)
+    assert start % rows == 0
     arrays = [*keeps, *[near_core(x) for x in gots]]
     extra = [] if carried is None else [carried]
 
@@ -320,15 +328,17 @@
     )(*[near_core(x) for x in parts], buffer)
 
 
-def inner_kernel(grad_rows, ids_ref, recv_ref, mixed_ref, factor_ref, *refs):
-    has_rows = grad_rows > 0
+def inner_kernel(grad_rows, sources, chip_ref, recv_ref, *refs):
+    mixed_refs = refs[:sources]
+    factor_ref = refs[sources]
+    out_ref = refs[-4] if grad_rows else refs[-2]
     rows_ref = refs[-1]
-    out_ref = refs[-4] if has_rows else refs[-2]
-    groups, per_block, width = mixed_ref.shape
+    groups, per_block, width = mixed_refs[0].shape
     size = factor_ref.shape[0]
     inner = size // groups
     outer = per_block // inner
-    start = pl.multiple_of(pl.program_id(0) * per_block, per_block)
+    step = pl.program_id(0)
+    start = pl.multiple_of(step * per_block, per_block)
     recv = recv_ref[:, pl.ds(start, per_block), :]
     rows_ref[...] = recv.reshape(groups * per_block, width).astype(F32)
     for i in range(0, outer, 2):
@@ -337,13 +347,16 @@
         ).astype(BF)
         back = jnp.dot(factor_ref[...], pair, preferred_element_type=F32)
         back = back.astype(BF).astype(F32)
-        residual = mixed_ref[:, i * inner : (i + 2) * inner, :].astype(F32)
+        rows = slice(i * inner, (i + 2) * inner)
+        residual = mixed_refs[0][:, rows, :].astype(F32)
+        for n, ref in enumerate(mixed_refs[1:], 1):
+            residual = jnp.where(step == n, ref[:, rows, :].astype(F32), residual)
         for n in range(2):
             own = residual[:, n * inner : (n + 1) * inner, :].reshape(size, width)
             out_ref[(i + n) * size : (i + n + 1) * size, :] = (
                 own + back[:, n * width : (n + 1) * width]
             ).astype(BF)
-    if has_rows:
+    if grad_rows:
         grads = recv_ref[:, recv_ref.shape[1] - grad_rows :, :].astype(F32)
         rows = grad_rows // 2
         for which in range(2):
@@ -351,33 +364,41 @@
             refs[-3 + which][...] = part.reshape(groups * rows, width)
 
 
-def inner_mix(block_ids, recv, mixed, factor_t, carried, per_block, grad_rows):
+def inner_mix(chip, begin, steps, recv, mixed, factor_t, carried, per_block, grad_rows):
     groups, _, width = recv.shape
-    steps = block_ids.shape[0]
-    spec = pl.BlockSpec((groups, per_block, width), lambda n, b: (0, n, 0))
     tokens = groups * per_block
     has_rows = carried is not None
-    extra = [carried] if has_rows else []
+    arrays = [array for array, _ in mixed]
+    single = len(mixed) == 1
+    mixed_specs = [
+        pl.BlockSpec(
+            (groups, per_block, width), lambda n, c, r=row: (0, n + r if single else r, 0)
+        )
+        for _, row in mixed
+    ]
     out_shape = [jax.ShapeDtypeStruct((tokens, NB * width), BF)]
-    out_specs = [pl.BlockSpec((tokens, width), lambda n, b: (0, b[n]))]
-    extra_specs = []
+    out_specs = [pl.BlockSpec((tokens, width), lambda n, c: (0, block_at(c, n + begin)))]
+    extra = []
     if has_rows:
-        extra_specs = [pl.BlockSpec(memory_space=pl.ANY)]
+        extra = [carried]
         full = (groups * grad_rows // 2, width)
         out_shape += [jax.ShapeDtypeStruct(full, F32)] * 2
-        out_specs += [pl.BlockSpec(full, lambda n, b: (0, 0))] * 2
-    return pl.pallas_call(
-        lambda *refs: inner_kernel(grad_rows if has_rows else 0, *refs),
+        out_specs += [pl.BlockSpec(full, lambda n, c: (0, 0))] * 2
+    return pl.pallas_call(
+        lambda *refs: inner_kernel(grad_rows if has_rows else 0, len(arrays), *refs),
         out_shape=out_shape,
         grid_spec=pltpu.PrefetchScalarGridSpec(
             num_scalar_prefetch=1,
             grid=(steps,),
-            in_specs=[WHOLE, spec, pl.BlockSpec(factor_t.shape, lambda n, b: (0, 0))] + extra_specs,
+            in_specs=[WHOLE]
+            + mixed_specs
+            + [pl.BlockSpec(factor_t.shape, lambda n, c: (0, 0))]
+            + [pl.BlockSpec(memory_space=pl.ANY)] * len(extra),
             out_specs=out_specs,
             scratch_shapes=[pltpu.VMEM((tokens, width), F32)],
         ),
-        input_output_aliases={4: 0} if has_rows else {},
-    )(block_ids, near_core(recv), mixed, factor_t, *extra)
+        input_output_aliases={3 + len(arrays): 0} if has_rows else {},
+    )(chip, near_core(recv), *arrays, factor_t, *extra)
 
 
 def shards(saved_mixed, out_grad, weight_in, weight_out, outer_factor, inner_factor, twiddle):
@@ -408,6 +429,7 @@
 
     offsets = (0, 1, 3, 2)
     ids = jnp.stack([(chip + offset) % NB for offset in offsets]).astype(jnp.int32)
+    chip_array = chip.reshape(1).astype(jnp.int32)
     pack = pack_shards(weight_in, weight_out, outer_factor, inner_factor)
     near = [pack]
     for n in range(1, NB):
@@ -417,16 +439,17 @@
         far.append(swap(near[n]))
     half_hidden = weight_in.shape[0]
     grad_rows = 2 * half_hidden // seq_devices
-    half_rows = (NB // 2) * per_block
-    rows_of = (half_rows, half_rows + NB * grad_rows)
-    calls = ((0, 1, 0, 0), (1, 2, 0, 1), (2, 4, 1, 0))
+    rest_rows = (NB - 1) * per_block
+    rows_of = (per_block, rest_rows + NB * grad_rows)
+    calls = ((0, 1, 0, 0), (1, 3, 1, 0), (3, 4, 1, 2))
     chunks = [None, None]
     keeps = []
     gots = []
     for begin, end, target, base in calls:
         pieces = [side[step] for step in range(begin, end) for side in (near, far)]
         chunks[target], keep, send = block_steps(
-            ids[begin:end],
+            chip_array,
+            begin,
             saved,
             upstream,
             pieces,
@@ -438,29 +461,38 @@
         )
         keeps.append(keep)
         gots.append(swap(send))
-    for n, group in enumerate((slice(0, 2), slice(2, 3))):
-        start = half_rows + n * 2 * grad_rows
+    done = 0
+    for group in (slice(0, 2), slice(2, 3)):
         chunks[1] = put_pair_sums(
-            keeps[group], gots[group], seq_devices, rows_of[1], start, chunks[1]
-        )
+            keeps[group],
+            gots[group],
+            seq_devices,
+            rows_of[1],
+            rest_rows + done * grad_rows,
+            chunks[1],
+        )
+        done += sum(keep.shape[0] for keep in keeps[group])
 
     factor_rows = outer_factor.shape[0]
     starts = jnp.concatenate([2 * ids + core, 2 * ids + 1 - core]).astype(jnp.int32) * factor_rows
     outer_t, inner_t = assemble_factors(starts, near + far, inner_size)
-    buffers = []
-    for half in range(2):
-        arrived = exchange(chunks[half])
-        buffers.append(
-            outer_mix(
-                arrived if half == 0 else near_core(arrived),
-                outer_t,
-                twiddle,
-                per_block,
-                NB // 2,
-                half_rows + half * grad_rows,
-            )
-        )
-    sums = seq_sums(arrived, NB * grad_rows, NB)
+    half_rows = (NB // 2) * per_block
+    arrivals = [exchange(chunks[n]) for n in range(2)]
+    mixes = ((0, 0, 1, 0, 0), (1, 0, 1, 0, 1), (1, 1, 2, 1, 0))
+    buffers = [None, None]
+    for source, first, steps, target, base in mixes:
+        buffers[target] = outer_mix(
+            arrivals[source] if source == 0 else near_core(arrivals[source]),
+            outer_t,
+            twiddle,
+            per_block,
+            first,
+            steps,
+            half_rows + target * grad_rows,
+            base,
+            buffers[target],
+        )
+    sums = seq_sums(arrivals[1], NB * grad_rows, NB)
     parts = [sums[0]]
     for n in range(1, NB):
         parts.append(from_chip(sums[n], -offsets[n]))
@@ -468,15 +500,9 @@
     second = spread_rows(parts, buffers[1], scale_factor)
     home.append(exchange(second))
     carried = None
-    for half in range(2):
+    for half, mixed in enumerate((((chunks[0], 0), (chunks[1], 0)), ((chunks[1], 1),))):
         outs = inner_mix(
-            ids[2 * half : 2 * half + 2],
-            home[half],
-            chunks[half],
-            inner_t,
-            carried,
-            per_block,
-            grad_rows,
+            chip_array, 2 * half, 2, home[half], mixed, inner_t, carried, per_block, grad_rows
         )
         carried = outs[0]
     input_grad = carried.reshape(seq_count, row_count, features)

time: 163 us -> 150 us (0.920)
  starting transfers between devices: 52.4 us -> 43.7 us
  waiting for transfers between devices: 61.9 us -> 60.2 us
    ppermute x6, waiting for transfers between devices: 31.5 us -> 20.8 us  [from_chip(): return lax.ppermute(piece, 'dp', pairs)]
    all_to_all x4, waiting for transfers between devices: 27.7 us -> 37 us  [exchange(): return lax.all_to_all(array, 'seq', split_axis=0, concat_axis=0, tiled=True)]
    ppermute x6, starting transfers between devices: 21.6 us -> 13.8 us  [from_chip(): return lax.ppermute(piece, 'dp', pairs)]
    pallas_call x4 -> x5, Pallas kernels: 12.8 us -> 13.2 us  [the longest x3 7.42 us: outer_mix(): pl.pallas_call(lambda *refs: outer_kernel(first, *refs), out_shape=jax.Sh...]
  transfers between devices with their start and end apart: 17 -> 17, of which waited for: 10 -> 10; matrix products, arithmetic and copies ran while one was open for 2% -> 1% of each run, Pallas kernels for 19% -> 20%
where the time goes in v3:
time: 150 us; the launch traced here: 149 us
  waiting for transfers between devices  60.2 us (40%)
  starting transfers between devices  43.7 us (29%)
  Pallas kernels  42.1 us (28%)
  local copies, waits for them, and re-layouts  1.64 us (1%)
    all_to_all x4, waiting for transfers between devices, exchange(): return lax.all_to_all(array, 'seq', split_axis=0, concat_axis=0, tiled=True)  37 us
    all_to_all x4, starting transfers between devices, exchange(): return lax.all_to_all(array, 'seq', split_axis=0, concat_axis=0, tiled=True)  29 us
    ppermute x6, waiting for transfers between devices, from_chip(): return lax.ppermute(piece, 'dp', pairs)  20.8 us
    pallas_call x3, Pallas kernels, block_steps(): pl.pallas_call(body, out_shape=out_shape, grid_spec=pltpu.PrefetchScalarG...  20.1 us
    ppermute x6, starting transfers between devices, from_chip(): return lax.ppermute(piece, 'dp', pairs)  13.8 us
    pallas_call x3, Pallas kernels, outer_mix(): pl.pallas_call(lambda *refs: outer_kernel(first, *refs), out_shape=jax.Sh...  7.42 us
    pallas_call x2, Pallas kernels, inner_mix(): pl.pallas_call(lambda *refs: inner_kernel(grad_rows if has_rows else 0, l...  5.76 us
    pallas_call x2, Pallas kernels, put_pair_sums(): pl.pallas_call(body, out_shape=jax.ShapeDtypeStruct((groups, total_rows,...  3.67 us
  transfers between devices with their start and end apart: 17, of which 10 were waited for; matrix products, arithmetic and copies ran while one was open for 1% of the time, Pallas kernels for 20%

profile of v3, /device:TPU:8, one launch (start us, length us, event | category | flops | bytes accessed | tf_op | source)
XLA Modules:
  0.0 149.1 jit_solution(7379305954983537331)
XLA Ops:
  3.8 5.5 %shard_map.96 = (bf16[32,64,128]{2,1,0:T(8,128)(2,1)}, f32[1,2,256,128]{3,2,1,0:T(8,128)}, f32[1,2,256,128]{3,2,1,0:T(8,128)}) custom-call(s32[1]{0:T(128)} %bitcast.refs_0_, bf16[2048,512]{1,0:T(8,128)(2,1)} %bitcast.8, bf16[2048,512]{1,0:T(8,128)(2,1)} %bitcast.11, bf16[640,128]{1,0:T(8,128)(2,1)} %pack.1.refs_3_.refs_0_, ...), custom_call_target="tpu_custom_call" | custom-call | tf_op jit(solution)/shard_map/pallas_call | solution.py:156
  9.3 8.9 %all-to-all-start.2 = ((bf16[32,64,128]{2,1,0:T(8,128)(2,1)}), bf16[32,64,128]{2,1,0:T(8,128)(2,1)S(1)}, u32[]{:S(2)}, u32[]{:S(2)}) async-start(bf16[32,64,128]{2,1,0:T(8,128)(2,1)} %get-tuple-element.35.refs_2_), calls=%async_computation.2 | async-start | bytes 1048576 | tf_op jit(solution)/shard_map/all_to_all | solution.py:428
  18.2 5.5 %collective-permute-start.2 = (bf16[640,128]{1,0:T(8,128)(2,1)S(1)}, bf16[640,128]{1,0:T(8,128)(2,1)S(1)}, u32[]{:S(2)}, u32[]{:S(2)}) collective-permute-start(bf16[640,128]{1,0:T(8,128)(2,1)S(1)} %copy-done.7), channel_id=1, source_target_pairs={{64,0},{96,32},{128,64},{160,96},{192,128},{224,160},{0,192},{32,2... | collective-permute-start | bytes 491528 | tf_op jit(solution)/shard_map/ppermute | solution.py:425
  23.7 3.2 %collective-permute-done.2.refs_3_.refs_1_ = bf16[640,128]{1,0:T(8,128)(2,1)S(1)} collective-permute-done((bf16[640,128]{1,0:T(8,128)(2,1)S(1)}, bf16[640,128]{1,0:T(8,128)(2,1)S(1)}, u32[]{:S(2)}, u32[]{:S(2)}) %collective-permute-start.2) | collective-permute-done | bytes 163872 | tf_op jit(solution)/shard_map/ppermute | solution.py:425
  26.9 9.8 %collective-permute-done.4.refs_5_.refs_2_ = bf16[640,128]{1,0:T(8,128)(2,1)S(1)} collective-permute-done((bf16[640,128]{1,0:T(8,128)(2,1)S(1)}, bf16[640,128]{1,0:T(8,128)(2,1)S(1)}, u32[]{:S(2)}, u32[]{:S(2)}) %collective-permute-start.4) | collective-permute-done | bytes 163872 | tf_op jit(solution)/shard_map/ppermute | solution.py:425
  38.2 9.0 %shard_map.94 = (bf16[32,256,128]{2,1,0:T(8,128)(2,1)}, f32[2,2,256,128]{3,2,1,0:T(8,128)}, f32[2,2,256,128]{3,2,1,0:T(8,128)}) custom-call(s32[1]{0:T(128)} %bitcast.refs_0_, bf16[2048,512]{1,0:T(8,128)(2,1)} %bitcast.9, bf16[2048,512]{1,0:T(8,128)(2,1)} %bitcast.12, bf16[640,128]{1,0:T(8,128)(2,1)} %copy-done.8, ...), custom_call_target="tpu_custom_call" | custom-call | tf_op jit(solution)/shard_map/pallas_call | solution.py:156
  47.5 3.1 %collective-permute-done.refs_3_ = bf16[640,128]{1,0:T(8,128)(2,1)S(1)} collective-permute-done((bf16[640,128]{1,0:T(8,128)(2,1)S(1)}, bf16[640,128]{1,0:T(8,128)(2,1)S(1)}, u32[]{:S(2)}, u32[]{:S(2)}) %collective-permute-start) | collective-permute-done | bytes 163872 | tf_op jit(solution)/shard_map/ppermute | solution.py:425
  52.0 5.7 %shard_map.95 = (bf16[32,256,128]{2,1,0:T(8,128)(2,1)}, f32[1,2,256,128]{3,2,1,0:T(8,128)}, f32[1,2,256,128]{3,2,1,0:T(8,128)}) custom-call(s32[1]{0:T(128)} %bitcast.refs_0_, bf16[2048,512]{1,0:T(8,128)(2,1)} %bitcast.10, bf16[2048,512]{1,0:T(8,128)(2,1)} %bitcast.13, bf16[640,128]{1,0:T(8,128)(2,1)} %copy-done.9, ...), custom_call_target="tpu_custom_call", output_to_operand_aliasing={{0}: (5, {})} | custom-call | tf_op jit(solution)/shard_map/pallas_call | solution.py:156
  57.8 2.0 %shard_map.97.refs_2_ = bf16[32,256,128]{2,1,0:T(8,128)(2,1)} custom-call(f32[1,2,256,128]{3,2,1,0:T(8,128)} %get-tuple-element.24.refs_0_, f32[2,2,256,128]{3,2,1,0:T(8,128)} %get-tuple-element.25.refs_1_, f32[1,2,256,128]{3,2,1,0:T(8,128)S(1)} %collective-permute-done.8.refs_2_, ...), custom_call_target="tpu_custom_call", output_to_operand_aliasing={{}: (4, {})} | custom-call | tf_op jit(solution)/shard_map/pallas_call | solution.py:277
  62.3 7.4 %all-to-all-start = ((bf16[32,256,128]{2,1,0:T(8,128)(2,1)}), bf16[32,256,128]{2,1,0:T(8,128)(2,1)S(1)}, u32[]{:S(2)}, u32[]{:S(2)}) async-start(bf16[32,256,128]{2,1,0:T(8,128)(2,1)} %shard_map.98.refs_3_.refs_2_), calls=%async_computation | async-start | bytes 4194304 | tf_op jit(solution)/shard_map/all_to_all | solution.py:428
  71.2 2.2 %factors.1 = (bf16[256,256]{1,0:T(8,128)(2,1)}, bf16[256,256]{1,0:T(8,128)(2,1)}) custom-call(s32[8]{0:T(128)} %add_multiply_fusion.1.rows_ref, bf16[640,128]{1,0:T(8,128)(2,1)} %pack.1.refs_3_.refs_0_, bf16[640,128]{1,0:T(8,128)(2,1)} %copy-done.8, bf16[640,128]{1,0:T(8,128)(2,1)} %copy-done.1, bf16[640,128]{1,0:T(8,128)(2,1)} %copy-done.9, ...), custom_call_target="tpu_custom_call" | custom-call | tf_op jit(solution)/shard_map/factors/pallas_call | solution.py:199
  73.4 2.4 %shard_map.102.refs_3_ = bf16[32,128,128]{2,1,0:T(8,128)(2,1)} custom-call(bf16[32,64,128]{2,1,0:T(8,128)(2,1)} %copy-done.6, bf16[256,256]{1,0:T(8,128)(2,1)} %get-tuple-element.33.refs_1_, f32[256,8]{1,0:T(8,128)} %copy.16.refs_2_), custom_call_target="tpu_custom_call" | custom-call | tf_op jit(solution)/shard_map/pallas_call | solution.py:235
  75.8 22.8 %all-to-all-done.parts_ref.refs_0_ = bf16[32,256,128]{2,1,0:T(8,128)(2,1)S(1)} async-done(((bf16[32,256,128]{2,1,0:T(8,128)(2,1)}), bf16[32,256,128]{2,1,0:T(8,128)(2,1)S(1)}, u32[]{:S(2)}, u32[]{:S(2)}) %all-to-all-start) | async-done | bytes 2097184 | tf_op jit(solution)/shard_map/all_to_all | solution.py:428
  98.7 2.2 %shard_map.103 = bf16[32,128,128]{2,1,0:T(8,128)(2,1)} custom-call(bf16[32,256,128]{2,1,0:T(8,128)(2,1)S(1)} %all-to-all-done.parts_ref.refs_0_, bf16[256,256]{1,0:T(8,128)(2,1)} %get-tuple-element.33.refs_1_, f32[256,8]{1,0:T(8,128)} %copy.16.refs_2_, bf16[32,128,128]{2,1,0:T(8,128)(2,1)} %shard_map.102.refs_3_), custom_call_target="tpu_custom_call", output_to_operand_aliasing={{}: (3, {})} | custom-call | tf_op jit(solution)/shard_map/pallas_call | solution.py:235
  100.9 5.5 %all-to-all-start.3 = ((bf16[32,128,128]{2,1,0:T(8,128)(2,1)}), bf16[32,128,128]{2,1,0:T(8,128)(2,1)S(1)}, u32[]{:S(2)}, u32[]{:S(2)}) async-start(bf16[32,128,128]{2,1,0:T(8,128)(2,1)} %shard_map.103), calls=%async_computation.3 | async-start | bytes 2097152 | tf_op jit(solution)/shard_map/all_to_all | solution.py:428
  107.1 2.4 %collective-permute-start.10 = (f32[16,128]{1,0:T(8,128)}, f32[16,128]{1,0:T(8,128)S(1)}, u32[]{:S(2)}, u32[]{:S(2)}) collective-permute-start(f32[16,128]{1,0:T(8,128)} %get-tuple-element.30), channel_id=1, source_target_pairs={{192,0},{224,32},{0,64},{32,96},{64,128},{96,160},{128,192},{160,2... | collective-permute-start | bytes 24584 | tf_op jit(solution)/shard_map/ppermute | solution.py:425
  109.5 1.7 %collective-permute-start.11 = (f32[16,128]{1,0:T(8,128)}, f32[16,128]{1,0:T(8,128)S(1)}, u32[]{:S(2)}, u32[]{:S(2)}) collective-permute-start(f32[16,128]{1,0:T(8,128)} %get-tuple-element.31), channel_id=1, source_target_pairs={{64,0},{96,32},{128,64},{160,96},{192,128},{224,160},{0,192},{32,2... | collective-permute-start | bytes 24584 | tf_op jit(solution)/shard_map/ppermute | solution.py:425
  111.2 2.7 %collective-permute-start.12 = (f32[16,128]{1,0:T(8,128)}, f32[16,128]{1,0:T(8,128)S(1)}, u32[]{:S(2)}, u32[]{:S(2)}) collective-permute-start(f32[16,128]{1,0:T(8,128)} %get-tuple-element.32), channel_id=1, source_target_pairs={{128,0},{160,32},{192,64},{224,96},{0,128},{32,160},{64,192},{96,2... | collective-permute-start | bytes 24584 | tf_op jit(solution)/shard_map/ppermute | solution.py:425
  113.9 2.8 %shard_map.100.refs_4_ = bf16[32,144,128]{2,1,0:T(8,128)(2,1)} custom-call(bf16[32,256,128]{2,1,0:T(8,128)(2,1)S(1)} %all-to-all-done.parts_ref.refs_0_, bf16[256,256]{1,0:T(8,128)(2,1)} %get-tuple-element.33.refs_1_, f32[256,8]{1,0:T(8,128)} %copy.16.refs_2_), custom_call_target="tpu_custom_call" | custom-call | tf_op jit(solution)/shard_map/pallas_call | solution.py:235
  116.7 4.5 %collective-permute-done.10.refs_1_ = f32[16,128]{1,0:T(8,128)S(1)} collective-permute-done((f32[16,128]{1,0:T(8,128)}, f32[16,128]{1,0:T(8,128)S(1)}, u32[]{:S(2)}, u32[]{:S(2)}) %collective-permute-start.10) | collective-permute-done | bytes 8224 | tf_op jit(solution)/shard_map/ppermute | solution.py:425
  123.0 7.2 %all-to-all-start.1 = ((bf16[32,144,128]{2,1,0:T(8,128)(2,1)}), bf16[32,144,128]{2,1,0:T(8,128)(2,1)S(1)}, u32[]{:S(2)}, u32[]{:S(2)}) async-start(bf16[32,144,128]{2,1,0:T(8,128)(2,1)} %shard_map.101), calls=%async_computation.1 | async-start | bytes 2359296 | tf_op jit(solution)/shard_map/all_to_all | solution.py:428
  130.2 3.0 %shard_map.104.refs_4_ = bf16[2048,512]{1,0:T(8,128)(2,1)} custom-call(s32[1]{0:T(128)} %bitcast.refs_0_, bf16[32,128,128]{2,1,0:T(8,128)(2,1)S(1)} %all-to-all-done.3.refs_1_, bf16[32,64,128]{2,1,0:T(8,128)(2,1)} %get-tuple-element.35.refs_2_, bf16[32,256,128]{2,1,0:T(8,128)(2,1)} %shard_map.98.refs_3_.refs_2_, ...), custom_call_target="tpu_custom_call" | custom-call | tf_op jit(solution)/shard_map/pallas_call | solution.py:387
  133.2 13.2 %all-to-all-done.1.refs_1_ = bf16[32,144,128]{2,1,0:T(8,128)(2,1)S(1)} async-done(((bf16[32,144,128]{2,1,0:T(8,128)(2,1)}), bf16[32,144,128]{2,1,0:T(8,128)(2,1)S(1)}, u32[]{:S(2)}, u32[]{:S(2)}) %all-to-all-start.1) | async-done | bytes 1179680 | tf_op jit(solution)/shard_map/all_to_all | solution.py:428
  146.4 2.8 %shard_map.105 = (bf16[2048,512]{1,0:T(8,128)(2,1)}, f32[256,128]{1,0:T(8,128)}, f32[256,128]{1,0:T(8,128)}) custom-call(s32[1]{0:T(128)} %bitcast.refs_0_, bf16[32,144,128]{2,1,0:T(8,128)(2,1)S(1)} %all-to-all-done.1.refs_1_, bf16[32,256,128]{2,1,0:T(8,128)(2,1)} %shard_map.98.refs_3_.refs_2_, ...), custom_call_target="tpu_custom_call", output_to_operand_aliasing={{0}: (4, {})} | custom-call | tf_op jit(solution)/shard_map/pallas_call | solution.py:387
  (52 shorter events, 12.9 us)
Async XLA Ops:
  2.2 1.6 %collective-permute-start.7 = (bf16[640,128]{1,0:T(8,128)(2,1)}, bf16[640,128]{1,0:T(8,128)(2,1)S(1)}, u32[]{:S(2)}, u32[]{:S(2)}) collective-permute-start(bf16[640,128]{1,0:T(8,128)(2,1)} %pack.1.refs_3_.refs_0_), channel_id=1, source_target_pairs={{0,32},{32,0},{64,96},{96,64},{128,160},{160,128},{192,224},{224,1... | collective-permute-start | bytes 491528 | tf_op jit(solution)/shard_map/ppermute | solution.py:421
  3.8 14.4 %copy-start.7 = (bf16[640,128]{1,0:T(8,128)(2,1)S(1)}, bf16[640,128]{1,0:T(8,128)(2,1)}, u32[]{:S(2)}) copy-start(bf16[640,128]{1,0:T(8,128)(2,1)} %pack.1.refs_3_.refs_0_) | copy-start | bytes 491524
  9.3 52.2 %all-to-all-start.2 = ((bf16[32,64,128]{2,1,0:T(8,128)(2,1)}), bf16[32,64,128]{2,1,0:T(8,128)(2,1)S(1)}, u32[]{:S(2)}, u32[]{:S(2)}) async-start(bf16[32,64,128]{2,1,0:T(8,128)(2,1)} %get-tuple-element.35.refs_2_), calls=%async_computation.2 | async-start | bytes 1048576 | tf_op jit(solution)/shard_map/all_to_all | solution.py:428
  18.2 32.4 %copy-start.11 = (f32[1,2,256,128]{3,2,1,0:T(8,128)S(1)}, f32[1,2,256,128]{3,2,1,0:T(8,128)}, u32[]{:S(2)}) copy-start(f32[1,2,256,128]{3,2,1,0:T(8,128)} %get-tuple-element.26) | copy-start | bytes 786436
  18.2 8.7 %collective-permute-start.2 = (bf16[640,128]{1,0:T(8,128)(2,1)S(1)}, bf16[640,128]{1,0:T(8,128)(2,1)S(1)}, u32[]{:S(2)}, u32[]{:S(2)}) collective-permute-start(bf16[640,128]{1,0:T(8,128)(2,1)S(1)} %copy-done.7), channel_id=1, source_target_pairs={{64,0},{96,32},{128,64},{160,96},{192,128},{224,160},{0,192},{32,2... | collective-permute-start | bytes 491528 | tf_op jit(solution)/shard_map/ppermute | solution.py:425
  23.7 13.1 %collective-permute-start.4 = (bf16[640,128]{1,0:T(8,128)(2,1)S(1)}, bf16[640,128]{1,0:T(8,128)(2,1)S(1)}, u32[]{:S(2)}, u32[]{:S(2)}) collective-permute-start(bf16[640,128]{1,0:T(8,128)(2,1)S(1)} %copy-done.7), channel_id=1, source_target_pairs={{192,0},{224,32},{0,64},{32,96},{64,128},{96,160},{128,192},{160,2... | collective-permute-start | bytes 491528 | tf_op jit(solution)/shard_map/ppermute | solution.py:425
  26.9 11.3 %copy-start.8 = (bf16[640,128]{1,0:T(8,128)(2,1)}, bf16[640,128]{1,0:T(8,128)(2,1)S(1)}, u32[]{:S(2)}) copy-start(bf16[640,128]{1,0:T(8,128)(2,1)S(1)} %collective-permute-done.2.refs_3_.refs_1_) | copy-start | bytes 491524
  26.9 11.3 %collective-permute-start.3 = (bf16[640,128]{1,0:T(8,128)(2,1)S(1)}, bf16[640,128]{1,0:T(8,128)(2,1)S(1)}, u32[]{:S(2)}, u32[]{:S(2)}) collective-permute-start(bf16[640,128]{1,0:T(8,128)(2,1)S(1)} %collective-permute-done.2.refs_3_.refs_1_), channel_id=1, source_target_pairs={{0,32},{32,0},{64,96},{96,64},{128,160},{160,128},{192,224},{224,1... | collective-permute-start | bytes 491528 | tf_op jit(solution)/shard_map/ppermute | solution.py:421
  36.7 10.4 %copy-start.1 = (bf16[640,128]{1,0:T(8,128)(2,1)}, bf16[640,128]{1,0:T(8,128)(2,1)S(1)}, u32[]{:S(2)}) copy-start(bf16[640,128]{1,0:T(8,128)(2,1)S(1)} %collective-permute-done.4.refs_5_.refs_2_) | copy-start | bytes 491524
  36.7 1.5 collective-permute-start.5
  36.7 13.8 %collective-permute-start = (bf16[640,128]{1,0:T(8,128)(2,1)S(1)}, bf16[640,128]{1,0:T(8,128)(2,1)S(1)}, u32[]{:S(2)}, u32[]{:S(2)}) collective-permute-start(bf16[640,128]{1,0:T(8,128)(2,1)S(1)} %copy-done.7), channel_id=1, source_target_pairs={{128,0},{160,32},{192,64},{224,96},{0,128},{32,160},{64,192},{96,2... | collective-permute-start | bytes 491528 | tf_op jit(solution)/shard_map/ppermute | solution.py:425
  38.2 9.0 %copy-start.2 = (bf16[640,128]{1,0:T(8,128)(2,1)}, bf16[640,128]{1,0:T(8,128)(2,1)S(1)}, u32[]{:S(2)}) copy-start(bf16[640,128]{1,0:T(8,128)(2,1)S(1)} %collective-permute-done.3.refs_4_.refs_5_) | copy-start | bytes 491524
  38.2 9.0 %copy-start.3 = (bf16[640,128]{1,0:T(8,128)(2,1)}, bf16[640,128]{1,0:T(8,128)(2,1)S(1)}, u32[]{:S(2)}) copy-start(bf16[640,128]{1,0:T(8,128)(2,1)S(1)} %collective-permute-done.5.refs_6_) | copy-start | bytes 491524
  47.2 10.6 %collective-permute-start.9 = (f32[2,2,256,128]{3,2,1,0:T(8,128)}, f32[2,2,256,128]{3,2,1,0:T(8,128)S(1)}, u32[]{:S(2)}, u32[]{:S(2)}) collective-permute-start(f32[2,2,256,128]{3,2,1,0:T(8,128)} %get-tuple-element.27), channel_id=1, source_target_pairs={{0,32},{32,0},{64,96},{96,64},{128,160},{160,128},{192,224},{224,1... | collective-permute-start | bytes 1572872 | tf_op jit(solution)/shard_map/ppermute | solution.py:421
  50.6 1.4 collective-permute-start.1
  50.6 7.2 %collective-permute-start.8 = (f32[1,2,256,128]{3,2,1,0:T(8,128)S(1)}, f32[1,2,256,128]{3,2,1,0:T(8,128)S(1)}, u32[]{:S(2)}, u32[]{:S(2)}) collective-permute-start(f32[1,2,256,128]{3,2,1,0:T(8,128)S(1)} %copy-done.11), channel_id=1, source_target_pairs={{0,32},{32,0},{64,96},{96,64},{128,160},{160,128},{192,224},{224,1... | collective-permute-start | bytes 786440 | tf_op jit(solution)/shard_map/ppermute | solution.py:421
  57.6 2.1 %collective-permute-start.6 = (f32[1,2,256,128]{3,2,1,0:T(8,128)}, f32[1,2,256,128]{3,2,1,0:T(8,128)S(1)}, u32[]{:S(2)}, u32[]{:S(2)}) collective-permute-start(f32[1,2,256,128]{3,2,1,0:T(8,128)} %get-tuple-element.23), channel_id=1, source_target_pairs={{0,32},{32,0},{64,96},{96,64},{128,160},{160,128},{192,224},{224,1... | collective-permute-start | bytes 786440 | tf_op jit(solution)/shard_map/ppermute | solution.py:421
  62.3 36.4 %all-to-all-start = ((bf16[32,256,128]{2,1,0:T(8,128)(2,1)}), bf16[32,256,128]{2,1,0:T(8,128)(2,1)S(1)}, u32[]{:S(2)}, u32[]{:S(2)}) async-start(bf16[32,256,128]{2,1,0:T(8,128)(2,1)} %shard_map.98.refs_3_.refs_2_), calls=%async_computation | async-start | bytes 4194304 | tf_op jit(solution)/shard_map/all_to_all | solution.py:428
  100.9 22.1 %all-to-all-start.3 = ((bf16[32,128,128]{2,1,0:T(8,128)(2,1)}), bf16[32,128,128]{2,1,0:T(8,128)(2,1)S(1)}, u32[]{:S(2)}, u32[]{:S(2)}) async-start(bf16[32,128,128]{2,1,0:T(8,128)(2,1)} %shard_map.103), calls=%async_computation.3 | async-start | bytes 2097152 | tf_op jit(solution)/shard_map/all_to_all | solution.py:428
  107.1 14.3 %copy-start.5 = (f32[16,128]{1,0:T(8,128)S(1)}, f32[16,128]{1,0:T(8,128)}, u32[]{:S(2)}) copy-start(f32[16,128]{1,0:T(8,128)} %get-tuple-element.29.refs_0_) | copy-start | bytes 24580
  107.1 14.1 %collective-permute-start.10 = (f32[16,128]{1,0:T(8,128)}, f32[16,128]{1,0:T(8,128)S(1)}, u32[]{:S(2)}, u32[]{:S(2)}) collective-permute-start(f32[16,128]{1,0:T(8,128)} %get-tuple-element.30), channel_id=1, source_target_pairs={{192,0},{224,32},{0,64},{32,96},{64,128},{96,160},{128,192},{160,2... | collective-permute-start | bytes 24584 | tf_op jit(solution)/shard_map/ppermute | solution.py:425
  109.5 11.7 %collective-permute-start.11 = (f32[16,128]{1,0:T(8,128)}, f32[16,128]{1,0:T(8,128)S(1)}, u32[]{:S(2)}, u32[]{:S(2)}) collective-permute-start(f32[16,128]{1,0:T(8,128)} %get-tuple-element.31), channel_id=1, source_target_pairs={{64,0},{96,32},{128,64},{160,96},{192,128},{224,160},{0,192},{32,2... | collective-permute-start | bytes 24584 | tf_op jit(solution)/shard_map/ppermute | solution.py:425
  111.2 10.1 %collective-permute-start.12 = (f32[16,128]{1,0:T(8,128)}, f32[16,128]{1,0:T(8,128)S(1)}, u32[]{:S(2)}, u32[]{:S(2)}) collective-permute-start(f32[16,128]{1,0:T(8,128)} %get-tuple-element.32), channel_id=1, source_target_pairs={{128,0},{160,32},{192,64},{224,96},{0,128},{32,160},{64,192},{96,2... | collective-permute-start | bytes 24584 | tf_op jit(solution)/shard_map/ppermute | solution.py:425
  123.0 23.3 %all-to-all-start.1 = ((bf16[32,144,128]{2,1,0:T(8,128)(2,1)}), bf16[32,144,128]{2,1,0:T(8,128)(2,1)S(1)}, u32[]{:S(2)}, u32[]{:S(2)}) async-start(bf16[32,144,128]{2,1,0:T(8,128)(2,1)} %shard_map.101), calls=%async_computation.1 | async-start | bytes 2359296 | tf_op jit(solution)/shard_map/all_to_all | solution.py:428
  (5 other events, 21.6 us)

commit v4 on v3

--- a/solution.py
+++ b/solution.py
@@ -439,9 +439,9 @@
         far.append(swap(near[n]))
     half_hidden = weight_in.shape[0]
     grad_rows = 2 * half_hidden // seq_devices
-    rest_rows = (NB - 1) * per_block
-    rows_of = (per_block, rest_rows + NB * grad_rows)
-    calls = ((0, 1, 0, 0), (1, 3, 1, 0), (3, 4, 1, 2))
+    half_rows = (NB // 2) * per_block
+    rows_of = (half_rows, half_rows + NB * grad_rows)
+    calls = ((0, 1, 0, 0), (1, 2, 0, 1), (2, 4, 1, 0))
     chunks = [None, None]
     keeps = []
     gots = []
@@ -468,7 +468,7 @@
             gots[group],
             seq_devices,
             rows_of[1],
-            rest_rows + done * grad_rows,
+            half_rows + done * grad_rows,
             chunks[1],
         )
         done += sum(keep.shape[0] for keep in keeps[group])
@@ -476,9 +476,8 @@
     factor_rows = outer_factor.shape[0]
     starts = jnp.concatenate([2 * ids + core, 2 * ids + 1 - core]).astype(jnp.int32) * factor_rows
     outer_t, inner_t = assemble_factors(starts, near + far, inner_size)
-    half_rows = (NB // 2) * per_block
     arrivals = [exchange(chunks[n]) for n in range(2)]
-    mixes = ((0, 0, 1, 0, 0), (1, 0, 1, 0, 1), (1, 1, 2, 1, 0))
+    mixes = ((0, 0, 2, 0, 0), (1, 0, 2, 1, 0))
     buffers = [None, None]
     for source, first, steps, target, base in mixes:
         buffers[target] = outer_mix(
@@ -500,7 +499,7 @@
     second = spread_rows(parts, buffers[1], scale_factor)
     home.append(exchange(second))
     carried = None
-    for half, mixed in enumerate((((chunks[0], 0), (chunks[1], 0)), ((chunks[1], 1),))):
+    for half, mixed in enumerate((((chunks[0], 0),), ((chunks[1], 0),))):
         outs = inner_mix(
             chip_array, 2 * half, 2, home[half], mixed, inner_t, carried, per_block, grad_rows
         )

time: 150 us -> 160 us (1.067)
  starting transfers between devices: 43.7 us -> 52.6 us
  waiting for transfers between devices: 60.2 us -> 63.6 us
  Pallas kernels: 42.1 us -> 40.4 us
    ppermute x6, waiting for transfers between devices: 20.8 us -> 31.4 us  [from_chip(): return lax.ppermute(piece, 'dp', pairs)]
    all_to_all x4, waiting for transfers between devices: 37 us -> 28.9 us  [exchange(): return lax.all_to_all(array, 'seq', split_axis=0, concat_axis=0, tiled=True)]
    ppermute x6, starting transfers between devices: 13.8 us -> 21.6 us  [from_chip(): return lax.ppermute(piece, 'dp', pairs)]
    pallas_call x3 -> x2, Pallas kernels: 7.42 us -> 5.89 us  [outer_mix(): pl.pallas_call(lambda *refs: outer_kernel(first, *refs), out_shape=jax.Sh...]
  transfers between devices with their start and end apart: 17 -> 17, of which waited for: 10 -> 10; matrix products, arithmetic and copies ran while one was open for 1% -> 1% of each run, Pallas kernels for 20% -> 19%
where the time goes in v4:
time: 160 us; the launch traced here: 159 us
  waiting for transfers between devices  63.6 us (40%)
  starting transfers between devices  52.6 us (33%)
  Pallas kernels  40.4 us (25%)
    ppermute x6, waiting for transfers between devices, from_chip(): return lax.ppermute(piece, 'dp', pairs)  31.4 us
    all_to_all x4, starting transfers between devices, exchange(): return lax.all_to_all(array, 'seq', split_axis=0, concat_axis=0, tiled=True)  29.7 us
    all_to_all x4, waiting for transfers between devices, exchange(): return lax.all_to_all(array, 'seq', split_axis=0, concat_axis=0, tiled=True)  28.9 us
    ppermute x6, starting transfers between devices, from_chip(): return lax.ppermute(piece, 'dp', pairs)  21.6 us
    pallas_call x3, Pallas kernels, block_steps(): pl.pallas_call(body, out_shape=out_shape, grid_spec=pltpu.PrefetchScalarG...  20.2 us
    pallas_call x2, Pallas kernels, outer_mix(): pl.pallas_call(lambda *refs: outer_kernel(first, *refs), out_shape=jax.Sh...  5.89 us
    pallas_call x2, Pallas kernels, inner_mix(): pl.pallas_call(lambda *refs: inner_kernel(grad_rows if has_rows else 0, l...  5.53 us
    pallas_call x2, Pallas kernels, put_pair_sums(): pl.pallas_call(body, out_shape=jax.ShapeDtypeStruct((groups, total_rows,...  3.65 us
  transfers between devices with their start and end apart: 17, of which 10 were waited for; matrix products, arithmetic and copies ran while one was open for 1% of the time, Pallas kernels for 19%

profile of v4, /device:TPU:8, one launch (start us, length us, event | category | flops | bytes accessed | tf_op | source)
XLA Modules:
  0.0 159.0 jit_solution(15347609826872064377)
XLA Ops:
  2.2 6.3 %collective-permute-start.6 = (bf16[640,128]{1,0:T(8,128)(2,1)}, bf16[640,128]{1,0:T(8,128)(2,1)S(1)}, u32[]{:S(2)}, u32[]{:S(2)}) collective-permute-start(bf16[640,128]{1,0:T(8,128)(2,1)} %pack.1.refs_3_.refs_0_), channel_id=1, source_target_pairs={{64,0},{96,32},{128,64},{160,96},{192,128},{224,160},{0,192},{32,2... | collective-permute-start | bytes 491528 | tf_op jit(solution)/shard_map/ppermute | solution.py:425
  8.5 7.3 %collective-permute-done.6.refs_3_.refs_1_ = bf16[640,128]{1,0:T(8,128)(2,1)S(1)} collective-permute-done((bf16[640,128]{1,0:T(8,128)(2,1)}, bf16[640,128]{1,0:T(8,128)(2,1)S(1)}, u32[]{:S(2)}, u32[]{:S(2)}) %collective-permute-start.6) | collective-permute-done | bytes 163872 | tf_op jit(solution)/shard_map/ppermute | solution.py:425
  15.8 5.7 %shard_map.95 = (bf16[32,128,128]{2,1,0:T(8,128)(2,1)}, f32[1,2,256,128]{3,2,1,0:T(8,128)}, f32[1,2,256,128]{3,2,1,0:T(8,128)}) custom-call(s32[1]{0:T(128)} %bitcast.refs_0_, bf16[2048,512]{1,0:T(8,128)(2,1)} %bitcast.8, bf16[2048,512]{1,0:T(8,128)(2,1)} %bitcast.11, bf16[640,128]{1,0:T(8,128)(2,1)} %pack.1.refs_3_.refs_0_, ...), custom_call_target="tpu_custom_call" | custom-call | tf_op jit(solution)/shard_map/pallas_call | solution.py:156
  21.5 5.6 %shard_map.96 = (bf16[32,128,128]{2,1,0:T(8,128)(2,1)}, f32[1,2,256,128]{3,2,1,0:T(8,128)}, f32[1,2,256,128]{3,2,1,0:T(8,128)}) custom-call(s32[1]{0:T(128)} %bitcast.refs_0_, bf16[2048,512]{1,0:T(8,128)(2,1)} %bitcast.9, bf16[2048,512]{1,0:T(8,128)(2,1)} %bitcast.12, bf16[640,128]{1,0:T(8,128)(2,1)} %copy-done.8, ...), custom_call_target="tpu_custom_call", output_to_operand_aliasing={{0}: (5, {})} | custom-call | tf_op jit(solution)/shard_map/pallas_call | solution.py:156
  27.1 7.7 %all-to-all-start.2 = ((bf16[32,128,128]{2,1,0:T(8,128)(2,1)}), bf16[32,128,128]{2,1,0:T(8,128)(2,1)S(1)}, u32[]{:S(2)}, u32[]{:S(2)}) async-start(bf16[32,128,128]{2,1,0:T(8,128)(2,1)} %get-tuple-element.35.refs_2_), calls=%async_computation.2 | async-start | bytes 2097152 | tf_op jit(solution)/shard_map/all_to_all | solution.py:428
  34.8 2.1 %collective-permute-start = (bf16[640,128]{1,0:T(8,128)(2,1)S(1)}, bf16[640,128]{1,0:T(8,128)(2,1)S(1)}, u32[]{:S(2)}, u32[]{:S(2)}) collective-permute-start(bf16[640,128]{1,0:T(8,128)(2,1)S(1)} %copy-done.7), channel_id=1, source_target_pairs={{192,0},{224,32},{0,64},{32,96},{64,128},{96,160},{128,192},{160,2... | collective-permute-start | bytes 491528 | tf_op jit(solution)/shard_map/ppermute | solution.py:425
  36.9 4.8 %collective-permute-start.2 = (bf16[640,128]{1,0:T(8,128)(2,1)S(1)}, bf16[640,128]{1,0:T(8,128)(2,1)S(1)}, u32[]{:S(2)}, u32[]{:S(2)}) collective-permute-start(bf16[640,128]{1,0:T(8,128)(2,1)S(1)} %copy-done.7), channel_id=1, source_target_pairs={{128,0},{160,32},{192,64},{224,96},{0,128},{32,160},{64,192},{96,2... | collective-permute-start | bytes 491528 | tf_op jit(solution)/shard_map/ppermute | solution.py:425
  41.7 20.9 %collective-permute-done.refs_3_.refs_2_ = bf16[640,128]{1,0:T(8,128)(2,1)S(1)} collective-permute-done((bf16[640,128]{1,0:T(8,128)(2,1)S(1)}, bf16[640,128]{1,0:T(8,128)(2,1)S(1)}, u32[]{:S(2)}, u32[]{:S(2)}) %collective-permute-start) | collective-permute-done | bytes 163872 | tf_op jit(solution)/shard_map/ppermute | solution.py:425
  64.3 8.9 %shard_map.94 = (bf16[32,192,128]{2,1,0:T(8,128)(2,1)}, f32[2,2,256,128]{3,2,1,0:T(8,128)}, f32[2,2,256,128]{3,2,1,0:T(8,128)}) custom-call(s32[1]{0:T(128)} %bitcast.refs_0_, bf16[2048,512]{1,0:T(8,128)(2,1)} %bitcast.10, bf16[2048,512]{1,0:T(8,128)(2,1)} %bitcast.13, bf16[640,128]{1,0:T(8,128)(2,1)} %copy-done.9, ...), custom_call_target="tpu_custom_call" | custom-call | tf_op jit(solution)/shard_map/pallas_call | solution.py:156
  76.2 1.8 %shard_map.97.refs_2_ = bf16[32,192,128]{2,1,0:T(8,128)(2,1)} custom-call(f32[1,2,256,128]{3,2,1,0:T(8,128)} %get-tuple-element.23.refs_0_, f32[1,2,256,128]{3,2,1,0:T(8,128)} %get-tuple-element.25.refs_1_, f32[1,2,256,128]{3,2,1,0:T(8,128)S(1)} %collective-permute-done.8.refs_2_, ...), custom_call_target="tpu_custom_call", output_to_operand_aliasing={{}: (4, {})} | custom-call | tf_op jit(solution)/shard_map/pallas_call | solution.py:277
  78.0 1.8 %shard_map.98.refs_2_ = bf16[32,192,128]{2,1,0:T(8,128)(2,1)} custom-call(f32[2,2,256,128]{3,2,1,0:T(8,128)} %get-tuple-element.21.refs_0_, f32[2,2,256,128]{3,2,1,0:T(8,128)S(1)} %collective-permute-done.4.refs_1_, bf16[32,192,128]{2,1,0:T(8,128)(2,1)} %shard_map.97.refs_2_), custom_call_target="tpu_custom_call", output_to_operand_aliasing={{}: (2, {})} | custom-call | tf_op jit(solution)/shard_map/pallas_call | solution.py:277
  79.9 7.5 %all-to-all-start = ((bf16[32,192,128]{2,1,0:T(8,128)(2,1)}), bf16[32,192,128]{2,1,0:T(8,128)(2,1)S(1)}, u32[]{:S(2)}, u32[]{:S(2)}) async-start(bf16[32,192,128]{2,1,0:T(8,128)(2,1)} %shard_map.98.refs_2_), calls=%async_computation | async-start | bytes 3145728 | tf_op jit(solution)/shard_map/all_to_all | solution.py:428
  89.0 2.2 %factors.1 = (bf16[256,256]{1,0:T(8,128)(2,1)}, bf16[256,256]{1,0:T(8,128)(2,1)}) custom-call(s32[8]{0:T(128)} %add_multiply_fusion.1.rows_ref, bf16[640,128]{1,0:T(8,128)(2,1)} %pack.1.refs_3_.refs_0_, bf16[640,128]{1,0:T(8,128)(2,1)} %copy-done.8, bf16[640,128]{1,0:T(8,128)(2,1)} %copy-done.9, bf16[640,128]{1,0:T(8,128)(2,1)} %copy-done.2, ...), custom_call_target="tpu_custom_call" | custom-call | tf_op jit(solution)/shard_map/factors/pallas_call | solution.py:199
  91.2 3.1 %shard_map.102 = bf16[32,128,128]{2,1,0:T(8,128)(2,1)} custom-call(bf16[32,128,128]{2,1,0:T(8,128)(2,1)} %copy-done.6, bf16[256,256]{1,0:T(8,128)(2,1)} %get-tuple-element.33.refs_1_, f32[256,8]{1,0:T(8,128)} %copy.15.refs_2_), custom_call_target="tpu_custom_call" | custom-call | tf_op jit(solution)/shard_map/pallas_call | solution.py:235
  94.3 15.7 %all-to-all-done.parts_ref.refs_0_ = bf16[32,192,128]{2,1,0:T(8,128)(2,1)S(1)} async-done(((bf16[32,192,128]{2,1,0:T(8,128)(2,1)}), bf16[32,192,128]{2,1,0:T(8,128)(2,1)S(1)}, u32[]{:S(2)}, u32[]{:S(2)}) %all-to-all-start) | async-done | bytes 1572896 | tf_op jit(solution)/shard_map/all_to_all | solution.py:428
  110.1 5.6 %all-to-all-start.3 = ((bf16[32,128,128]{2,1,0:T(8,128)(2,1)}), bf16[32,128,128]{2,1,0:T(8,128)(2,1)S(1)}, u32[]{:S(2)}, u32[]{:S(2)}) async-start(bf16[32,128,128]{2,1,0:T(8,128)(2,1)} %shard_map.102), calls=%async_computation.3 | async-start | bytes 2097152 | tf_op jit(solution)/shard_map/all_to_all | solution.py:428
  116.3 4.8 %collective-permute-start.10 = (f32[16,128]{1,0:T(8,128)}, f32[16,128]{1,0:T(8,128)S(1)}, u32[]{:S(2)}, u32[]{:S(2)}) collective-permute-start(f32[16,128]{1,0:T(8,128)} %get-tuple-element.30), channel_id=1, source_target_pairs={{192,0},{224,32},{0,64},{32,96},{64,128},{96,160},{128,192},{160,2... | collective-permute-start | bytes 24584 | tf_op jit(solution)/shard_map/ppermute | solution.py:425
  121.1 3.6 %collective-permute-start.12 = (f32[16,128]{1,0:T(8,128)}, f32[16,128]{1,0:T(8,128)S(1)}, u32[]{:S(2)}, u32[]{:S(2)}) collective-permute-start(f32[16,128]{1,0:T(8,128)} %get-tuple-element.32), channel_id=1, source_target_pairs={{128,0},{160,32},{192,64},{224,96},{0,128},{32,160},{64,192},{96,2... | collective-permute-start | bytes 24584 | tf_op jit(solution)/shard_map/ppermute | solution.py:425
  124.7 2.8 %shard_map.100.refs_4_ = bf16[32,144,128]{2,1,0:T(8,128)(2,1)} custom-call(bf16[32,192,128]{2,1,0:T(8,128)(2,1)S(1)} %all-to-all-done.parts_ref.refs_0_, bf16[256,256]{1,0:T(8,128)(2,1)} %get-tuple-element.33.refs_1_, f32[256,8]{1,0:T(8,128)} %copy.15.refs_2_), custom_call_target="tpu_custom_call" | custom-call | tf_op jit(solution)/shard_map/pallas_call | solution.py:235
  127.5 3.2 %collective-permute-done.10.refs_1_ = f32[16,128]{1,0:T(8,128)S(1)} collective-permute-done((f32[16,128]{1,0:T(8,128)}, f32[16,128]{1,0:T(8,128)S(1)}, u32[]{:S(2)}, u32[]{:S(2)}) %collective-permute-start.10) | collective-permute-done | bytes 8224 | tf_op jit(solution)/shard_map/ppermute | solution.py:425
  131.9 8.9 %all-to-all-start.1 = ((bf16[32,144,128]{2,1,0:T(8,128)(2,1)}), bf16[32,144,128]{2,1,0:T(8,128)(2,1)S(1)}, u32[]{:S(2)}, u32[]{:S(2)}) async-start(bf16[32,144,128]{2,1,0:T(8,128)(2,1)} %shard_map.101), calls=%async_computation.1 | async-start | bytes 2359296 | tf_op jit(solution)/shard_map/all_to_all | solution.py:428
  140.9 2.8 %shard_map.103.refs_4_ = bf16[2048,512]{1,0:T(8,128)(2,1)} custom-call(s32[1]{0:T(128)} %bitcast.refs_0_, bf16[32,128,128]{2,1,0:T(8,128)(2,1)S(1)} %all-to-all-done.3.refs_1_, bf16[32,128,128]{2,1,0:T(8,128)(2,1)} %get-tuple-element.35.refs_2_, bf16[256,256]{1,0:T(8,128)(2,1)} %get-tuple-element.34.refs_3_), custom_call_target="tpu_custom_call" | custom-call | tf_op jit(solution)/shard_map/pallas_call | solution.py:387
  143.6 12.6 %all-to-all-done.1.refs_1_ = bf16[32,144,128]{2,1,0:T(8,128)(2,1)S(1)} async-done(((bf16[32,144,128]{2,1,0:T(8,128)(2,1)}), bf16[32,144,128]{2,1,0:T(8,128)(2,1)S(1)}, u32[]{:S(2)}, u32[]{:S(2)}) %all-to-all-start.1) | async-done | bytes 1179680 | tf_op jit(solution)/shard_map/all_to_all | solution.py:428
  156.2 2.8 %shard_map.104 = (bf16[2048,512]{1,0:T(8,128)(2,1)}, f32[256,128]{1,0:T(8,128)}, f32[256,128]{1,0:T(8,128)}) custom-call(s32[1]{0:T(128)} %bitcast.refs_0_, bf16[32,144,128]{2,1,0:T(8,128)(2,1)S(1)} %all-to-all-done.1.refs_1_, bf16[32,192,128]{2,1,0:T(8,128)(2,1)} %shard_map.98.refs_2_, ...), custom_call_target="tpu_custom_call", output_to_operand_aliasing={{0}: (4, {})} | custom-call | tf_op jit(solution)/shard_map/pallas_call | solution.py:387
  (53 shorter events, 9.7 us)
Async XLA Ops:
  2.2 13.6 %collective-permute-start.6 = (bf16[640,128]{1,0:T(8,128)(2,1)}, bf16[640,128]{1,0:T(8,128)(2,1)S(1)}, u32[]{:S(2)}, u32[]{:S(2)}) collective-permute-start(bf16[640,128]{1,0:T(8,128)(2,1)} %pack.1.refs_3_.refs_0_), channel_id=1, source_target_pairs={{64,0},{96,32},{128,64},{160,96},{192,128},{224,160},{0,192},{32,2... | collective-permute-start | bytes 491528 | tf_op jit(solution)/shard_map/ppermute | solution.py:425
  8.5 7.3 %collective-permute-start.5 = (bf16[640,128]{1,0:T(8,128)(2,1)}, bf16[640,128]{1,0:T(8,128)(2,1)S(1)}, u32[]{:S(2)}, u32[]{:S(2)}) collective-permute-start(bf16[640,128]{1,0:T(8,128)(2,1)} %pack.1.refs_3_.refs_0_), channel_id=1, source_target_pairs={{0,32},{32,0},{64,96},{96,64},{128,160},{160,128},{192,224},{224,1... | collective-permute-start | bytes 491528 | tf_op jit(solution)/shard_map/ppermute | solution.py:421
  15.8 5.7 %collective-permute-start.7 = (bf16[640,128]{1,0:T(8,128)(2,1)S(1)}, bf16[640,128]{1,0:T(8,128)(2,1)S(1)}, u32[]{:S(2)}, u32[]{:S(2)}) collective-permute-start(bf16[640,128]{1,0:T(8,128)(2,1)S(1)} %collective-permute-done.6.refs_3_.refs_1_), channel_id=1, source_target_pairs={{0,32},{32,0},{64,96},{96,64},{128,160},{160,128},{192,224},{224,1... | collective-permute-start | bytes 491528 | tf_op jit(solution)/shard_map/ppermute | solution.py:421
  27.1 7.7 %copy-start.7 = (bf16[640,128]{1,0:T(8,128)(2,1)S(1)}, bf16[640,128]{1,0:T(8,128)(2,1)}, u32[]{:S(2)}) copy-start(bf16[640,128]{1,0:T(8,128)(2,1)} %pack.1.refs_3_.refs_0_) | copy-start | bytes 491524
  27.1 52.8 %all-to-all-start.2 = ((bf16[32,128,128]{2,1,0:T(8,128)(2,1)}), bf16[32,128,128]{2,1,0:T(8,128)(2,1)S(1)}, u32[]{:S(2)}, u32[]{:S(2)}) async-start(bf16[32,128,128]{2,1,0:T(8,128)(2,1)} %get-tuple-element.35.refs_2_), calls=%async_computation.2 | async-start | bytes 2097152 | tf_op jit(solution)/shard_map/all_to_all | solution.py:428
  34.8 38.8 %copy-start.11 = (f32[1,2,256,128]{3,2,1,0:T(8,128)S(1)}, f32[1,2,256,128]{3,2,1,0:T(8,128)}, u32[]{:S(2)}) copy-start(f32[1,2,256,128]{3,2,1,0:T(8,128)} %get-tuple-element.26) | copy-start | bytes 786436
  34.8 39.1 %copy-start.12 = (f32[1,2,256,128]{3,2,1,0:T(8,128)S(1)}, f32[1,2,256,128]{3,2,1,0:T(8,128)}, u32[]{:S(2)}) copy-start(f32[1,2,256,128]{3,2,1,0:T(8,128)} %get-tuple-element.27) | copy-start | bytes 786436
  34.8 27.8 %collective-permute-start = (bf16[640,128]{1,0:T(8,128)(2,1)S(1)}, bf16[640,128]{1,0:T(8,128)(2,1)S(1)}, u32[]{:S(2)}, u32[]{:S(2)}) collective-permute-start(bf16[640,128]{1,0:T(8,128)(2,1)S(1)} %copy-done.7), channel_id=1, source_target_pairs={{192,0},{224,32},{0,64},{32,96},{64,128},{96,160},{128,192},{160,2... | collective-permute-start | bytes 491528 | tf_op jit(solution)/shard_map/ppermute | solution.py:425
  36.9 25.7 %collective-permute-start.2 = (bf16[640,128]{1,0:T(8,128)(2,1)S(1)}, bf16[640,128]{1,0:T(8,128)(2,1)S(1)}, u32[]{:S(2)}, u32[]{:S(2)}) collective-permute-start(bf16[640,128]{1,0:T(8,128)(2,1)S(1)} %copy-done.7), channel_id=1, source_target_pairs={{128,0},{160,32},{192,64},{224,96},{0,128},{32,160},{64,192},{96,2... | collective-permute-start | bytes 491528 | tf_op jit(solution)/shard_map/ppermute | solution.py:425
  62.6 1.4 collective-permute-start.1
  62.6 10.6 %copy-start.2 = (bf16[640,128]{1,0:T(8,128)(2,1)}, bf16[640,128]{1,0:T(8,128)(2,1)S(1)}, u32[]{:S(2)}) copy-start(bf16[640,128]{1,0:T(8,128)(2,1)S(1)} %collective-permute-done.2.refs_5_.refs_3_) | copy-start | bytes 491524
  62.7 1.7 %collective-permute-start.3 = (bf16[640,128]{1,0:T(8,128)(2,1)S(1)}, bf16[640,128]{1,0:T(8,128)(2,1)S(1)}, u32[]{:S(2)}, u32[]{:S(2)}) collective-permute-start(bf16[640,128]{1,0:T(8,128)(2,1)S(1)} %collective-permute-done.2.refs_5_.refs_3_), channel_id=1, source_target_pairs={{0,32},{32,0},{64,96},{96,64},{128,160},{160,128},{192,224},{224,1... | collective-permute-start | bytes 491528 | tf_op jit(solution)/shard_map/ppermute | solution.py:421
  64.0 9.2 %copy-start.3 = (bf16[640,128]{1,0:T(8,128)(2,1)}, bf16[640,128]{1,0:T(8,128)(2,1)S(1)}, u32[]{:S(2)}) copy-start(bf16[640,128]{1,0:T(8,128)(2,1)S(1)} %collective-permute-done.1.refs_4_.refs_6_) | copy-start | bytes 491524
  64.3 8.9 %copy-start.4 = (bf16[640,128]{1,0:T(8,128)(2,1)}, bf16[640,128]{1,0:T(8,128)(2,1)S(1)}, u32[]{:S(2)}) copy-start(bf16[640,128]{1,0:T(8,128)(2,1)S(1)} %collective-permute-done.3.refs_6_.refs_7_) | copy-start | bytes 491524
  73.2 4.8 %collective-permute-start.4 = (f32[2,2,256,128]{3,2,1,0:T(8,128)}, f32[2,2,256,128]{3,2,1,0:T(8,128)S(1)}, u32[]{:S(2)}, u32[]{:S(2)}) collective-permute-start(f32[2,2,256,128]{3,2,1,0:T(8,128)} %get-tuple-element.22), channel_id=1, source_target_pairs={{0,32},{32,0},{64,96},{96,64},{128,160},{160,128},{192,224},{224,1... | collective-permute-start | bytes 1572872 | tf_op jit(solution)/shard_map/ppermute | solution.py:421
  73.6 2.3 %collective-permute-start.8 = (f32[1,2,256,128]{3,2,1,0:T(8,128)S(1)}, f32[1,2,256,128]{3,2,1,0:T(8,128)S(1)}, u32[]{:S(2)}, u32[]{:S(2)}) collective-permute-start(f32[1,2,256,128]{3,2,1,0:T(8,128)S(1)} %copy-done.11), channel_id=1, source_target_pairs={{0,32},{32,0},{64,96},{96,64},{128,160},{160,128},{192,224},{224,1... | collective-permute-start | bytes 786440 | tf_op jit(solution)/shard_map/ppermute | solution.py:421
  73.9 2.4 %collective-permute-start.9 = (f32[1,2,256,128]{3,2,1,0:T(8,128)S(1)}, f32[1,2,256,128]{3,2,1,0:T(8,128)S(1)}, u32[]{:S(2)}, u32[]{:S(2)}) collective-permute-start(f32[1,2,256,128]{3,2,1,0:T(8,128)S(1)} %copy-done.12), channel_id=1, source_target_pairs={{0,32},{32,0},{64,96},{96,64},{128,160},{160,128},{192,224},{224,1... | collective-permute-start | bytes 786440 | tf_op jit(solution)/shard_map/ppermute | solution.py:421
  79.9 30.2 %all-to-all-start = ((bf16[32,192,128]{2,1,0:T(8,128)(2,1)}), bf16[32,192,128]{2,1,0:T(8,128)(2,1)S(1)}, u32[]{:S(2)}, u32[]{:S(2)}) async-start(bf16[32,192,128]{2,1,0:T(8,128)(2,1)} %shard_map.98.refs_2_), calls=%async_computation | async-start | bytes 3145728 | tf_op jit(solution)/shard_map/all_to_all | solution.py:428
  110.1 21.9 %all-to-all-start.3 = ((bf16[32,128,128]{2,1,0:T(8,128)(2,1)}), bf16[32,128,128]{2,1,0:T(8,128)(2,1)S(1)}, u32[]{:S(2)}, u32[]{:S(2)}) async-start(bf16[32,128,128]{2,1,0:T(8,128)(2,1)} %shard_map.102), calls=%async_computation.3 | async-start | bytes 2097152 | tf_op jit(solution)/shard_map/all_to_all | solution.py:428
  116.3 14.4 %copy-start.5 = (f32[16,128]{1,0:T(8,128)S(1)}, f32[16,128]{1,0:T(8,128)}, u32[]{:S(2)}) copy-start(f32[16,128]{1,0:T(8,128)} %get-tuple-element.29.refs_0_) | copy-start | bytes 24580
  116.3 14.3 %collective-permute-start.10 = (f32[16,128]{1,0:T(8,128)}, f32[16,128]{1,0:T(8,128)S(1)}, u32[]{:S(2)}, u32[]{:S(2)}) collective-permute-start(f32[16,128]{1,0:T(8,128)} %get-tuple-element.30), channel_id=1, source_target_pairs={{192,0},{224,32},{0,64},{32,96},{64,128},{96,160},{128,192},{160,2... | collective-permute-start | bytes 24584 | tf_op jit(solution)/shard_map/ppermute | solution.py:425
  121.1 9.6 %collective-permute-start.11 = (f32[16,128]{1,0:T(8,128)}, f32[16,128]{1,0:T(8,128)S(1)}, u32[]{:S(2)}, u32[]{:S(2)}) collective-permute-start(f32[16,128]{1,0:T(8,128)} %get-tuple-element.31), channel_id=1, source_target_pairs={{64,0},{96,32},{128,64},{160,96},{192,128},{224,160},{0,192},{32,2... | collective-permute-start | bytes 24584 | tf_op jit(solution)/shard_map/ppermute | solution.py:425
  121.1 9.6 %collective-permute-start.12 = (f32[16,128]{1,0:T(8,128)}, f32[16,128]{1,0:T(8,128)S(1)}, u32[]{:S(2)}, u32[]{:S(2)}) collective-permute-start(f32[16,128]{1,0:T(8,128)} %get-tuple-element.32), channel_id=1, source_target_pairs={{128,0},{160,32},{192,64},{224,96},{0,128},{32,160},{64,192},{96,2... | collective-permute-start | bytes 24584 | tf_op jit(solution)/shard_map/ppermute | solution.py:425
  131.9 24.3 %all-to-all-start.1 = ((bf16[32,144,128]{2,1,0:T(8,128)(2,1)}), bf16[32,144,128]{2,1,0:T(8,128)(2,1)S(1)}, u32[]{:S(2)}, u32[]{:S(2)}) async-start(bf16[32,144,128]{2,1,0:T(8,128)(2,1)} %shard_map.101), calls=%async_computation.1 | async-start | bytes 2359296 | tf_op jit(solution)/shard_map/all_to_all | solution.py:428
  (6 other events, 33.8 us)
